TPU v7x, 128 devices: a whole 4x4x4 slice. The times are simulated.
128 devices in a mesh: head: 4 (over z_lo, core), track: 32 (over y, z_hi, x).
Axes of the slice: x: 4, y: 4, z: 4 (z_hi: 2, z_lo: 2; z = z_hi * 2 + z_lo), core: 2. Of those that a mesh axis runs over, the one named last changes fastest.
Arguments:
- potential: float32 [256, 4096, 128], P('head', 'track'), may hold values from -6 to 6
- source: float32 [256, 4096, 128], P('head', 'track'), may hold values from -6 to 6
- depth_kernel: float32 [3, 128], replicated, may hold values from -0.5 to 0.5
- magnet: float32 [3, 32, 16384], P(None, 'track', 'head'), may hold values from -0.8 to 0.8
- footprint: int32 [32, 16384], P('track', 'head'), may hold values from 0 to 262143, as said below
- temp_index: int32 [32, 16384], P('track', 'head'), may hold values from 0 to 127
- temp_profile: float32 [128], replicated, may hold values from 0.3 to 1.4
- self_tiles: float32 [32, 128, 128, 128], P('track', 'head'), may hold values from -0.5 to 0.5
- next_tiles: float32 [32, 128, 128, 128], P('track', 'head'), may hold values from -0.5 to 0.5
Outputs:
- relaxed: float32 [256, 4096, 128], P('head', 'track')
- magnet_out: float32 [3, 32, 16384], P(None, 'track', 'head')
Inputs may be any that keep to these rules, and one draw needn't show every extreme that they name: Within the 4096 grains of one device (an aligned block of a track tile), no more than 256 have footprint cells in any one pole block of 8192 cells; in every draw one pole block, the same for every device, takes exactly 256 grains of every device.
All inputs are finite; a program needn't handle non-finite values.
Results may differ from a plain program's by a relative error of at most 0.0001.
Values sent between devices are 32-bit elements; how exact they have to be, the bound alone decides.
A program may use at most 320 MiB of HBM per device.

v0:
```python
import jax
import jax.numpy as jnp
from jax import lax
from jax.sharding import PartitionSpec as P

HIGH = lax.Precision.HIGHEST


def extended(block, sides, width):
    for axis, dim in sides:
        count = lax.axis_size(axis)
        forward = [(i, i + 1) for i in range(count - 1)]
        backward = [(target, source) for source, target in forward]
        low = lax.ppermute(
            lax.slice_in_dim(block, block.shape[dim] - width, None, axis=dim), axis, forward
        )
        high = lax.ppermute(lax.slice_in_dim(block, 0, width, axis=dim), axis, backward)
        block = jnp.concatenate([low, block, high], axis=dim)
    return block


def relax_sweep(padded, source):
    center = padded[1:-1, 1:-1]
    deep = jnp.pad(center, ((0, 0), (0, 0), (1, 1)))
    others = [
        padded[2:, 1:-1],
        padded[:-2, 1:-1],
        padded[1:-1, 2:],
        padded[1:-1, :-2],
        deep[:, :, 2:],
        deep[:, :, :-2],
    ]
    numer = source
    denom = jnp.ones_like(center)
    for other in others:
        differ = other - center
        perm = 1.0 + 4.0 / (1.0 + 4.0 * differ * differ)
        numer = numer + perm * differ
        denom = denom + perm
    return center + 0.8 * numer / denom


def cross_comp(a_vec, b_vec):
    return jnp.stack(
        [
            a_vec[1] * b_vec[2] - a_vec[2] * b_vec[1],
            a_vec[2] * b_vec[0] - a_vec[0] * b_vec[2],
            a_vec[0] * b_vec[1] - a_vec[1] * b_vec[0],
        ]
    )


def llb_section(state, field, target):
    sq_norm = jnp.sum(state * state, axis=0)
    total = field + 0.5 * (1.0 - sq_norm / target) * state
    turn = cross_comp(state, total)
    damp = cross_comp(state, turn)
    along = jnp.sum(state * total, axis=0)
    return state + 0.1 * (-turn - 0.5 * damp + 0.3 * along * state)


def per_device(
    potential,
    source,
    depth_kernel,
    magnet,
    footprint,
    temp_index,
    temp_profile,
    self_tiles,
    next_tiles,
):
    rows_x, rows_y, depth = potential.shape
    relaxed = potential
    for sweep_idx in range(2):
        padded = extended(relaxed, (("head", 0), ("track", 1)), 1)
        relaxed = relax_sweep(padded, source)
    surface = jnp.einsum("kz,xyz->kxy", depth_kernel, relaxed, precision=HIGH).reshape(
        3, rows_x * rows_y
    )
    cells = footprint[0]
    table = lax.all_gather(surface, "track", axis=1, tiled=True)
    applied = jnp.take(table, cells, axis=1)
    n_prof = temp_profile.shape[0]
    onehot = (temp_index[0][None, :] == jnp.arange(n_prof, dtype=jnp.int32)[:, None]).astype(
        jnp.float32
    )
    temp = jnp.dot(temp_profile[None, :], onehot, precision=HIGH)[0]
    target = 0.05 + jnp.maximum(1.0 - temp, 0.0)
    couple_self = self_tiles[0]
    couple_next = next_tiles[0]
    n_tiles, tile_w = (couple_self.shape[0], couple_self.shape[1])
    state = magnet[:, 0, :]
    for section in range(2):
        rimmed = extended(state, (("head", 1),), tile_w)
        tiles = rimmed.reshape(3, n_tiles + 2, tile_w)
        ex = jnp.einsum("kij,ckj->cki", couple_self, tiles[:, 1:-1], precision=HIGH)
        ex = ex + jnp.einsum("kij,ckj->cki", couple_next, tiles[:, :-2], precision=HIGH)
        ex = ex + jnp.einsum("kji,ckj->cki", couple_next, tiles[:, 2:], precision=HIGH)
        state = llb_section(state, applied + ex.reshape(3, n_tiles * tile_w), target)
    return (relaxed, state[:, None, :])


def solution(mesh):
    in_specs = (
        P("head", "track", None),
        P("head", "track", None),
        P(),
        P(None, "track", "head"),
        P("track", "head"),
        P("track", "head"),
        P(),
        P("track", "head", None, None),
        P("track", "head", None, None),
    )
    out_specs = (P("head", "track", None), P(None, "track", "head"))
    return jax.shard_map(
        per_device, mesh=mesh, in_specs=in_specs, out_specs=out_specs, check_vma=False
    )
```

profile of v0, /device:TPU:1, one launch (start us, length us, event | category | flops | bytes accessed | tf_op | source)
XLA Modules:
  0.0 1086.3 jit_solution(5104642623732953517)
XLA Ops:
  7.2 1.0 fusion.118
  8.2 4.9 collective-permute-start.1
  13.2 1.9 collective-permute-start
  15.2 2.6 constant_dynamic-update-slice_fusion.1
  18.8 1.4 collective-permute-start.2
  20.3 4.0 collective-permute-start.3
  24.3 1.0 collective-permute-done.3
  25.3 12.3 %divide_add_fusion.1 = f32[64,128,128]{2,1,0:T(8,128)S(1)} fusion(f32[64,128,128]{2,1,0:T(8,128)S(1)} %copy-done.1, f32[66,128,128]{2,1,0:T(8,128)S(1)} %constant_dynamic-update-slice_fusion, f32[66,1,128]{2,1,0:T(1,128)S(1)} %collective-permute-done.3, f32[66,1,128]{2,1,0:T(1,128)S(1)} %collective-permute-done.2, ...), kind=kLoop, calls=%fused_computation.77 | loop fusion | flops 63963136 | bytes 17106944 | tf_op jit(solution)/shard_map/add | solution.py:40
  37.6 1.9 collective-permute-start.4
  39.5 3.9 collective-permute-start.5
  43.5 1.3 collective-permute-done.5
  44.8 1.3 collective-permute-start.6
  46.2 4.6 collective-permute-start.7
  51.7 14.4 %divide_add_fusion = f32[64,128,128]{2,1,0:T(8,128)S(1)} fusion(f32[64,128,128]{2,1,0:T(8,128)S(1)} %divide_add_fusion.1, f32[1,128,128]{2,1,0:T(8,128)S(1)} %collective-permute-done.4, f32[1,128,128]{2,1,0:T(8,128)S(1)} %collective-permute-done.5, f32[66,1,128]{2,1,0:T(1,128)S(1)} %collective-permute-done.7, f32[66,1,128]{2,1,0:T(1,128)S(1)} %collective-permute-done.6, ...), kind=kLoop, calls=%fused_computation.76 | loop fusion | flops 68157440 | bytes 12781568 | tf_op jit(solution)/shard_map/add | solution.py:40
  66.2 2.0 copy-done.3
  68.2 3.6 convolution_bitcast_fusion
  71.8 2.6 copy.106
  74.6 5.1 collective-permute-start.8
  79.7 2.1 collective-permute-start.9
  82.7 1.8 collective-permute-done.9
  84.6 1.9 fusion.50
  86.4 3.3 fusion.52
  89.8 904.3 %all-gather.2.cloned.1.call-done = f32[3,262144]{0,1:T(8,128)} async-done(((f32[3,8192]{0,1:T(8,128)}), f32[3,262144]{0,1:T(8,128)}) %all-gather.2.cloned.1.call-update) | async-done | bytes 3145744 | tf_op jit(solution)/shard_map/all_gather | solution.py:82
  994.1 59.8 %gather_fusion = f32[4096,3]{1,0:T(8,128)} fusion(f32[3,262144]{0,1:T(8,128)} %all-gather.2.cloned.1.call-done, s32[4096]{0:T(1024)S(1)} %broadcast_clamp_fusion), kind=kCustom, calls=%fused_computation | custom fusion | bytes 114688 | tf_op jit(solution)/shard_map/jit(_take)/gather | solution.py:83
  1053.9 2.2 copy.107
  1056.1 5.0 multiply_reduce_fusion.2
  1061.5 3.4 collective-permute-start.10
  1064.9 2.1 collective-permute-start.11
  1067.1 2.7 collective-permute-done.11
  1069.8 3.3 fusion.48
  1073.1 1.9 fusion.46
  1075.0 3.4 multiply_reduce_fusion
  (54 shorter events, 4.6 us)
Async XLA Ops:
  7.2 77.4 %copy-start = (f32[1,32,128,128]{3,2,1,0:T(8,128)S(1)}, f32[1,32,128,128]{3,2,1,0:T(8,128)}, u32[]{:S(2)}) copy-start(f32[1,32,128,128]{3,2,1,0:T(8,128)} %param.17) | copy-start | bytes 6291460
  7.2 986.9 %all-gather.2.cloned.1.call-start = ((), (), s32[]{:S(2)}) async-start(), calls=%async_computation | async-start | bytes 138412032 | tf_op jit(solution)/shard_map/all_gather | solution.py:82
  8.2 6.9 collective-permute-start.1
  13.2 5.6 collective-permute-start
  15.1 10.1 copy-start.1
  15.2 10.1 copy-start.2
  18.8 5.4 collective-permute-start.2
  20.3 5.0 collective-permute-start.3
  37.6 5.9 collective-permute-start.4
  39.5 5.3 collective-permute-start.5
  44.8 5.9 collective-permute-start.6
  46.1 22.0 %copy-start.7 = (f32[3,128]{1,0:T(4,128)S(1)}, f32[3,128]{1,0:T(4,128)}, u32[]{:S(2)}) copy-start(f32[3,128]{1,0:T(4,128)} %param.11) | copy-start | bytes 4612
  46.2 5.6 collective-permute-start.7
  66.1 2.0 copy-start.3
  71.8 2.7 copy-start.5
  71.8 10.1 copy-start.6
  71.8 10.1 copy-start.8
  71.8 10.1 copy-start.9
  74.6 8.2 collective-permute-start.8
  79.7 4.9 collective-permute-start.9
  1061.1 13.9 %copy-start.4 = (f32[1,32,128,128]{3,2,1,0:T(8,128)S(1)}, f32[1,32,128,128]{3,2,1,0:T(8,128)}, u32[]{:S(2)}) copy-start(f32[1,32,128,128]{3,2,1,0:T(8,128)} %param.16) | copy-start | bytes 6291460
  1061.5 5.6 collective-permute-start.10
  1064.9 4.9 collective-permute-start.11
Sparse Core Ops, SparseCore 0:
  74.6 919.3 all-gather.1
where the time goes:
time: 1090 us
  waiting for transfers between devices  913 us (84%)
  local copies, waits for them, and re-layouts  70.5 us (6%)
  starting transfers between devices  36.8 us (3%)
  other arithmetic  28.2 us (3%)
  matrix products  23.2 us (2%)
  between operations  14.5 us (1%)
    all_gather x1, waiting for transfers between devices, per_device(): table = lax.all_gather(surface, 'track', axis=1, tiled=True)  904 us
    gather x2, local copies, waits for them, and re-layouts, per_device(): applied = jnp.take(table, cells, axis=1)  62 us
    add x2, other arithmetic, relax_sweep(): return center + 0.8 * numer / denom  26.7 us
    ppermute x6, starting transfers between devices, extended(): lax.ppermute(lax.slice_in_dim(block, block.shape[dim] - width, None, axis...  26 us
  transfers between devices with their start and end apart: 13, of which 7 were waited for; matrix products, arithmetic and copies ran while one was open for 1% of the time, Pallas kernels for 0%

commit v1 on v0

v1 whole, which is shorter than its diff:
```python
import functools

import jax
import jax.numpy as jnp
from jax import lax
from jax.experimental import pallas as pl
from jax.experimental.pallas import tpu as pltpu
from jax.sharding import PartitionSpec as P

F32 = jnp.float32
BF16 = jnp.bfloat16
I32 = jnp.int32
NN = (((1,), (0,)), ((), ()))
NT = (((1,), (1,)), ((), ()))
ROW0 = 8


def mxu(a, b, dims):
    return lax.dot_general(a, b, dims, preferred_element_type=F32)


def split(a):
    high = a.astype(BF16)
    return high, (a - high.astype(F32)).astype(BF16)


def face(a, b):
    differ = b - a
    perm = 1.0 + pltpu.reciprocal(0.25 + differ * differ)
    return perm, perm * differ


def relax_rows(lower, center, upper, before, after, drive, carried, first, last):
    perm, flux = face(center, upper)
    numer = (drive - carried[1]) + flux
    denom = (1.0 + carried[0]) + perm
    carried = (perm, flux)
    perm, flux = face(before, center)
    numer = numer - flux
    denom = denom + perm
    depth = center.shape[1]
    for other in (
        after,
        jnp.where(last, 0.0, pltpu.roll(center, depth - 1, 1)),
        jnp.where(first, 0.0, pltpu.roll(center, 1, 1)),
    ):
        perm, flux = face(center, other)
        numer = numer + flux
        denom = denom + perm
    return center + (0.8 * numer) * pltpu.reciprocal(denom), carried


def one_hot_rows(index, count):
    lanes = index.shape[1]
    rows = lax.broadcasted_iota(I32, (count, lanes), 0)
    return jnp.where(rows == jnp.broadcast_to(index, (count, lanes)), 1.0, 0.0)


def lookup(table, address):
    hot = jnp.concatenate([one_hot_rows(a & 127, 128) for a in address], axis=1).astype(BF16)
    found = mxu(table, jnp.concatenate([hot, hot], axis=0), NN)
    results = []
    for part, a in enumerate(address):
        group = jnp.broadcast_to(a >> 8, (8, 128))
        odd = jnp.broadcast_to((a >> 7) & 1, (8, 128))
        total = jnp.zeros((8, 128), F32)
        for g in range(table.shape[0] // 8):
            total = total + jnp.where(
                group == g, found[8 * g : 8 * g + 8, 128 * part : 128 * part + 128], 0.0
            )
        results.append(jnp.where(odd == 0, total, pltpu.roll(total, 7, 0)))
    return results


def halves(rows):
    high, low = split(rows)
    return jnp.concatenate([high, low], axis=1)


def llb_section(state, field, target):
    mx, my, mz = state
    sq_norm = mx * mx + my * my + mz * mz
    pull = 0.5 * (1.0 - sq_norm / target)
    hx, hy, hz = (f + pull * m for f, m in zip(field, state))
    tx, ty, tz = my * hz - mz * hy, mz * hx - mx * hz, mx * hy - my * hx
    dx, dy, dz = my * tz - mz * ty, mz * tx - mx * tz, mx * ty - my * tx
    along = 0.3 * (mx * hx + my * hy + mz * hz)
    return tuple(
        m + 0.1 * (along * m - t - 0.5 * d)
        for m, t, d in zip(state, (tx, ty, tz), (dx, dy, dz))
    )


def kernel(
    n_head,
    n_track,
    pot_hbm,
    src_hbm,
    dk_hbm,
    mag_hbm,
    foot_hbm,
    temp_hbm,
    prof_hbm,
    self_hbm,
    next_hbm,
    out_hbm,
    mout_hbm,
    pot,
    mid,
    src,
    dk,
    mag,
    foot,
    tidx,
    prof,
    tself,
    tnext,
    self_high,
    self_low,
    next_high,
    next_low,
    lhs,
    ex,
    rim,
    rim_new,
    edge,
    addr,
    ask,
    asked,
    surf,
    answer,
    answered,
    field,
    in_sem,
    out_sem,
    halo_send,
    halo_recv,
    mid_send,
    mid_recv,
    rim_send,
    rim_recv,
    ask_send,
    ask_recv,
    ans_send,
    ans_recv,
):
    head = lax.axis_index("head")
    track = lax.axis_index("track")
    n_x, n_y = src.shape[0], src.shape[1]
    n_tiles = mag.shape[1]
    inner = pl.ds(ROW0, n_y)

    has_low_x, has_high_x = head > 0, head < n_head - 1
    has_low_y, has_high_y = track > 0, track < n_track - 1
    low_x, high_x = (head - 1, track), (head + 1, track)
    low_y, high_y = (head, track - 1), (head, track + 1)

    def partner(step):
        return lax.rem(track + step, n_track)

    loads = [
        pltpu.make_async_copy(a, b, in_sem.at[i])
        for i, (a, b) in enumerate(
            [
                (foot_hbm, foot),
                (pot_hbm, pot.at[pl.ds(1, n_x), inner, :]),
                (src_hbm, src),
                (mag_hbm, mag),
                (dk_hbm, dk),
                (temp_hbm, tidx),
                (prof_hbm, prof),
                (self_hbm, tself),
                (next_hbm, tnext),
            ]
        )
    ]
    for copy in loads:
        copy.start()

    for ref in (pot, mid):
        for plane in (0, n_x + 1):
            ref[plane, ROW0 : ROW0 + n_y, :] = jnp.zeros((n_y, ref.shape[2]), F32)
        for row in (ROW0 - 1, ROW0 + n_y):
            ref[1 : n_x + 1, row : row + 1, :] = jnp.zeros((n_x, 1, ref.shape[2]), F32)
    rim[...] = jnp.zeros(rim.shape, F32)
    rim_new[...] = jnp.zeros(rim_new.shape, F32)

    barrier = pltpu.get_barrier_semaphore()

    def greet(step, _):
        pl.semaphore_signal(barrier, inc=1, device_id=(head, partner(step)), device_id_type=pl.DeviceIdType.MESH)
        return 0

    lax.fori_loop(1, n_track, greet, 0)
    for there, device in ((has_low_x, low_x), (has_high_x, high_x)):

        @pl.when(there)
        def _():
            pl.semaphore_signal(barrier, inc=1, device_id=device, device_id_type=pl.DeviceIdType.MESH)

    n_greeted = n_track - 1 + has_low_x.astype(I32) + has_high_x.astype(I32)
    pl.semaphore_wait(barrier, n_greeted)

    def remote(a, b, send, recv, device):
        return pltpu.make_async_remote_copy(
            src_ref=a, dst_ref=b, send_sem=send, recv_sem=recv, device_id=device,
            device_id_type=pl.DeviceIdType.MESH,
        )

    def brick_halo(source, first, row, target, send, recv):
        rows, planes = pl.ds(row, n_y), pl.ds(first, n_x)
        all_x = pl.ds(1, n_x)
        return [
            (has_low_x, remote(source.at[first, rows, :], target.at[n_x + 1, inner, :], send.at[0], recv.at[1], low_x)),
            (has_high_x, remote(source.at[first + n_x - 1, rows, :], target.at[0, inner, :], send.at[1], recv.at[0], high_x)),
            (has_low_y, remote(source.at[planes, pl.ds(row, 1), :], target.at[all_x, pl.ds(ROW0 + n_y, 1), :], send.at[2], recv.at[3], low_y)),
            (has_high_y, remote(source.at[planes, pl.ds(row + n_y - 1, 1), :], target.at[all_x, pl.ds(ROW0 - 1, 1), :], send.at[3], recv.at[2], high_y)),
        ]

    def brick_wait(source, first, row, target, send, recv):
        rows, planes = pl.ds(row, n_y), pl.ds(first, n_x)
        all_x = pl.ds(1, n_x)
        waits = [
            (has_low_x, remote(source.at[first, rows, :], target.at[0, inner, :], send.at[0], recv.at[0], low_x)),
            (has_high_x, remote(source.at[first, rows, :], target.at[n_x + 1, inner, :], send.at[1], recv.at[1], high_x)),
            (has_low_y, remote(source.at[planes, pl.ds(row, 1), :], target.at[all_x, pl.ds(ROW0 - 1, 1), :], send.at[2], recv.at[2], low_y)),
            (has_high_y, remote(source.at[planes, pl.ds(row, 1), :], target.at[all_x, pl.ds(ROW0 + n_y, 1), :], send.at[3], recv.at[3], high_y)),
        ]
        for there, copy in waits:

            @pl.when(there)
            def _():
                copy.wait_send()
                copy.wait_recv()

    def start(copies):
        for there, copy in copies:

            @pl.when(there)
            def _():
                copy.start()

    start(brick_halo(pot_hbm, 0, 0, pot, halo_send, halo_recv))
    loads[3].wait()

    def rim_copies(source, target, slot):
        return [
            (has_low_x, remote(source.at[0], target.at[1], rim_send.at[slot], rim_recv.at[slot + 1], low_x)),
            (has_high_x, remote(source.at[1], target.at[0], rim_send.at[slot + 1], rim_recv.at[slot], high_x)),
        ]

    def rim_wait(source, target, slot):
        for i, (there, device) in enumerate(((has_low_x, low_x), (has_high_x, high_x))):

            @pl.when(there)
            def _():
                copy = remote(source.at[i], target.at[i], rim_send.at[slot + i], rim_recv.at[slot + i], device)
                copy.wait_send()
                copy.wait_recv()

    def put_edges(slot, state):
        edge[slot] = jnp.zeros((2, 8, 128), F32)
        for comp, value in enumerate(state):
            edge[slot, 0, comp : comp + 1, :] = value[0:1, :]
            edge[slot, 1, comp : comp + 1, :] = value[n_tiles - 1 : n_tiles, :]

    state = [mag[comp] for comp in range(3)]
    put_edges(0, state)
    start(rim_copies(edge.at[0], rim, 0))

    loads[0].wait()
    later = lax.broadcasted_iota(I32, (128, 128), 0) < lax.broadcasted_iota(I32, (128, 128), 1)
    count_matrix = jnp.concatenate(
        [jnp.where(later, 1.0, 0.0), jnp.ones((128, 128), F32)], axis=1
    ).astype(BF16)
    before = jnp.zeros((n_track, 128), F32)
    asks = jnp.zeros((128, 128), F32)
    for chunk in range(n_tiles):
        cell = foot[chunk : chunk + 1, :]
        owner = cell >> 13
        hot = one_hot_rows(owner, n_track)
        counts = mxu(hot.astype(BF16), count_matrix, NN)
        place = jnp.sum(hot * (counts[:, :128] + before), axis=0, keepdims=True).astype(I32)
        before = before + counts[:, 128:]
        where_at = owner * 256 + place
        addr[chunk : chunk + 1, :] = where_at
        row = one_hot_rows(where_at >> 7, 2 * n_track)
        lane = one_hot_rows(where_at & 127, 128)
        high = jnp.broadcast_to((cell >> 7) & 63, row.shape).astype(F32)
        low = jnp.broadcast_to(cell & 127, row.shape).astype(F32)
        values = jnp.concatenate([row * high, row * low], axis=0)
        asks = asks + mxu(values.astype(BF16), lane.astype(BF16), NT)
    ask[...] = jnp.zeros(ask.shape, I32)
    cells = (asks[: 2 * n_track] * 128.0 + asks[2 * n_track :]).astype(I32)
    for owner in range(n_track):
        ask[owner, 0:2, :] = cells[2 * owner : 2 * owner + 2, :]

    def send_ask(step, _):
        other = partner(step)
        remote(ask.at[other], asked.at[track], ask_send.at[other], ask_recv.at[track], (head, other)).start()
        return 0

    own_ask = pltpu.make_async_copy(ask.at[track], asked.at[track], ask_send.at[track])
    own_ask.start()
    lax.fori_loop(1, n_track, send_ask, 0)

    loads[1].wait()
    loads[2].wait()
    brick_wait(pot_hbm, 0, 0, pot, halo_send, halo_recv)

    rows_at = 32
    lanes = lax.broadcasted_iota(I32, (rows_at, 128), 1)
    first, last = lanes == 0, lanes == 127

    def plane(source, x, row, carried):
        o = ROW0 + row
        rows = slice(o, o + rows_at)
        return relax_rows(
            None,
            source[x + 1, rows, :],
            source[x + 2, rows, :],
            source[x + 1, o - 1 : o - 1 + rows_at, :],
            source[x + 1, o + 1 : o + 1 + rows_at, :],
            src[x, row : row + rows_at, :],
            carried,
            first,
            last,
        )

    for row in range(0, n_y, rows_at):
        rows = slice(ROW0 + row, ROW0 + row + rows_at)

        def step(x, carried):
            mid[x + 1, rows, :], carried = plane(pot, x, row, carried)
            return carried

        lax.fori_loop(0, n_x, step, face(pot[0, rows, :], pot[1, rows, :]), unroll=8)

    start(brick_halo(mid, 1, ROW0, mid, mid_send, mid_recv))

    def set_lhs(tile, value, comp):
        high = value.astype(BF16).astype(F32)
        lhs[pl.ds(16 * tile + comp, value.shape[0], stride=16), :] = high
        lhs[pl.ds(16 * tile + 8 + comp, value.shape[0], stride=16), :] = value - high

    lhs[...] = jnp.zeros(lhs.shape, F32)
    loads[7].wait()
    loads[8].wait()
    rim_wait(edge.at[0], rim, 0)
    for comp in range(3):
        set_lhs(1, state[comp], comp)
        lhs[comp : comp + 1, :] = rim[0, comp : comp + 1, :].astype(BF16).astype(F32)
        lhs[8 + comp : 9 + comp, :] = rim[0, comp : comp + 1, :] - lhs[comp : comp + 1, :]
        at = 16 * (n_tiles + 1) + comp
        lhs[at : at + 1, :] = rim[1, comp : comp + 1, :].astype(BF16).astype(F32)
        lhs[at + 8 : at + 9, :] = rim[1, comp : comp + 1, :] - lhs[at : at + 1, :]

    def split_tile(k, _):
        self_high[k], self_low[k] = split(tself[k])
        next_high[k], next_low[k] = split(tnext[k])
        return 0

    lax.fori_loop(0, n_tiles, split_tile, 0, unroll=2)

    def get_lhs(tile):
        return lhs[pl.ds(pl.multiple_of(16 * tile, 16), 16), :].astype(BF16)

    def fold(parts):
        return parts[:8] + parts[8:]

    def exchange(k, _):
        own, low, high = get_lhs(k + 1), get_lhs(k), get_lhs(k + 2)
        parts = mxu(own, self_high[k], NT) + mxu(own, self_low[k], NT)
        parts = parts + (mxu(low, next_high[k], NT) + mxu(low, next_low[k], NT))
        parts = parts + (mxu(high, next_high[k], NN) + mxu(high, next_low[k], NN))
        ex[pl.ds(pl.multiple_of(8 * k, 8), 8), :] = fold(parts)
        return 0

    lax.fori_loop(0, n_tiles, exchange, 0, unroll=4)

    def get_ex(comp):
        return ex[pl.ds(comp, n_tiles, stride=8), :]

    first_ex = [get_ex(comp) for comp in range(3)]
    for comp in range(3):
        field[comp] = first_ex[comp]

    loads[4].wait()
    rows8 = lax.broadcasted_iota(I32, (8, 128), 0)
    kernels = []
    for odd in range(2):
        weights = jnp.zeros((8, 128), F32)
        for comp in range(3):
            weights = weights + jnp.where(
                rows8 == 2 * comp + odd, jnp.broadcast_to(dk[comp : comp + 1, :], (8, 128)), 0.0
            )
        high = weights.astype(BF16).astype(F32)
        kernels.append(jnp.concatenate([high, weights - high], axis=0).astype(BF16))

    brick_wait(mid, 1, ROW0, mid, mid_send, mid_recv)

    for row in range(0, n_y, rows_at):
        rows = slice(ROW0 + row, ROW0 + row + rows_at)

        def step2(x, carried):
            pot[x + 1, rows, :], carried = plane(mid, x, row, carried)
            return carried

        lax.fori_loop(0, n_x, step2, face(mid[0, rows, :], mid[1, rows, :]), unroll=8)

    store = pltpu.make_async_copy(pot.at[pl.ds(1, n_x), inner, :], out_hbm, out_sem.at[0])
    store.start()

    def surface(pair, _):
        total = jnp.zeros((8, 128), F32)
        for odd in range(2):
            high, low = split(pot[2 * pair + odd + 1, ROW0 : ROW0 + n_y, :])
            total = total + fold(mxu(kernels[odd], high, NT)) + fold(mxu(kernels[odd], low, NT))
        surf[pl.ds(pl.multiple_of(8 * pair, 8), 8), :] = total
        return 0

    lax.fori_loop(0, n_x // 2, surface, 0, unroll=4)

    own_ask.wait()

    def wait_ask(step, _):
        other = partner(step)
        copy = remote(ask.at[other], asked.at[other], ask_send.at[other], ask_recv.at[other], (head, other))
        copy.wait_send()
        copy.wait_recv()
        return 0

    lax.fori_loop(1, n_track, wait_ask, 0)
    table = halves(surf[...])

    def reply(step, _):
        other = partner(step)
        low, high = lookup(table, [asked[other, 0:1, :], asked[other, 1:2, :]])
        answer[other] = jnp.where(rows8 % 2 == 0, low, pltpu.roll(high, 1, 0))

        @pl.when(step > 0)
        def _():
            remote(answer.at[other], answered.at[track], ans_send.at[other], ans_recv.at[track], (head, other)).start()

        return 0

    lax.fori_loop(0, n_track, reply, 0)
    own_answer = pltpu.make_async_copy(answer.at[track], answered.at[track], ans_send.at[track])
    own_answer.start()
    own_answer.wait()

    loads[5].wait()
    loads[6].wait()
    profile = jnp.broadcast_to(prof[...], (8, 128))
    temp = jnp.concatenate(
        [
            jnp.take_along_axis(profile, tidx[at : at + 8, :], axis=1)
            for at in range(0, n_tiles, 8)
        ],
        axis=0,
    )
    target = 0.05 + jnp.maximum(1.0 - temp, 0.0)

    def wait_answer(step, _):
        other = partner(step)
        copy = remote(answer.at[other], answered.at[other], ans_send.at[other], ans_recv.at[other], (head, other))
        copy.wait_send()
        copy.wait_recv()
        return 0

    lax.fori_loop(1, n_track, wait_answer, 0)
    table = halves(answered[...].reshape(8 * n_track, 128))

    applied = [[] for _ in range(3)]
    for pair in range(n_tiles // 2):
        found = lookup(table, [addr[2 * pair + i : 2 * pair + i + 1, :] for i in range(2)])
        for value in found:
            for comp in range(3):
                applied[comp].append(value[2 * comp : 2 * comp + 1, :])
    applied = [jnp.concatenate(rows, axis=0) for rows in applied]

    state = llb_section(state, [a + field[comp] for comp, a in enumerate(applied)], target)
    put_edges(1, state)
    start(rim_copies(edge.at[1], rim_new, 2))

    lhs[0:16, :] = jnp.zeros((16, 128), F32)
    lhs[16 * (n_tiles + 1) :, :] = jnp.zeros((16, 128), F32)
    for comp in range(3):
        set_lhs(1, state[comp], comp)
    lax.fori_loop(0, n_tiles, exchange, 0, unroll=4)
    rim_wait(edge.at[1], rim_new, 2)
    end = n_tiles - 1
    for side, tile, dims in ((0, 0, NT), (1, end, NN)):
        high = rim_new[side].astype(BF16).astype(F32)
        both = jnp.concatenate([high, rim_new[side] - high], axis=0).astype(BF16)
        parts = mxu(both, next_high[tile], dims) + mxu(both, next_low[tile], dims)
        ex[8 * tile : 8 * tile + 8, :] = ex[8 * tile : 8 * tile + 8, :] + fold(parts)
    state = llb_section(state, [a + get_ex(comp) for comp, a in enumerate(applied)], target)
    for comp in range(3):
        mag[comp] = state[comp]
    result = pltpu.make_async_copy(mag, mout_hbm, out_sem.at[1])
    result.start()
    result.wait()
    store.wait()


def per_device(n_head, n_track, potential, source, depth_kernel, magnet, footprint, temp_index, temp_profile, self_tiles, next_tiles):
    n_x, n_y, n_z = potential.shape
    n_tiles, width = self_tiles.shape[1], self_tiles.shape[2]
    any_space = pl.BlockSpec(memory_space=pl.ANY)
    dma = pltpu.SemaphoreType.DMA
    relaxed, magnet_out = pl.pallas_call(
        functools.partial(kernel, n_head, n_track),
        out_shape=(
            jax.ShapeDtypeStruct(potential.shape, F32),
            jax.ShapeDtypeStruct((3, n_tiles, width), F32),
        ),
        in_specs=[any_space] * 9,
        out_specs=(any_space, any_space),
        scratch_shapes=[
            pltpu.VMEM((n_x + 2, n_y + 16, n_z), F32),
            pltpu.VMEM((n_x + 2, n_y + 16, n_z), F32),
            pltpu.VMEM((n_x, n_y, n_z), F32),
            pltpu.VMEM((3, n_z), F32),
            pltpu.VMEM((3, n_tiles, width), F32),
            pltpu.VMEM((n_tiles, width), I32),
            pltpu.VMEM((n_tiles, width), I32),
            pltpu.VMEM((1, 128), F32),
            pltpu.VMEM((n_tiles, width, width), F32),
            pltpu.VMEM((n_tiles, width, width), F32),
            pltpu.VMEM((n_tiles, width, width), BF16),
            pltpu.VMEM((n_tiles, width, width), BF16),
            pltpu.VMEM((n_tiles, width, width), BF16),
            pltpu.VMEM((n_tiles, width, width), BF16),
            pltpu.VMEM((16 * (n_tiles + 2), width), F32),
            pltpu.VMEM((8 * n_tiles, width), F32),
            pltpu.VMEM((2, 8, width), F32),
            pltpu.VMEM((2, 8, width), F32),
            pltpu.VMEM((2, 2, 8, width), F32),
            pltpu.VMEM((n_tiles, width), I32),
            pltpu.VMEM((n_track, 8, 128), I32),
            pltpu.VMEM((n_track, 8, 128), I32),
            pltpu.VMEM((8 * (n_x // 2), 128), F32),
            pltpu.VMEM((n_track, 8, 128), F32),
            pltpu.VMEM((n_track, 8, 128), F32),
            pltpu.VMEM((3, n_tiles, width), F32),
            dma((9,)),
            dma((2,)),
            dma((4,)),
            dma((4,)),
            dma((4,)),
            dma((4,)),
            dma((4,)),
            dma((4,)),
            dma((n_track,)),
            dma((n_track,)),
            dma((n_track,)),
            dma((n_track,)),
        ],
        compiler_params=pltpu.CompilerParams(
            collective_id=0, has_side_effects=True, vmem_limit_bytes=48 << 20
        ),
        name="pole_and_grains",
    )(
        potential,
        source,
        depth_kernel,
        magnet.reshape(3, n_tiles, width),
        footprint.reshape(n_tiles, width),
        temp_index.reshape(n_tiles, width),
        temp_profile.reshape(1, -1),
        self_tiles[0],
        next_tiles[0],
    )
    return relaxed, magnet_out.reshape(magnet.shape)


def solution(mesh):
    in_specs = (
        P("head", "track", None),
        P("head", "track", None),
        P(),
        P(None, "track", "head"),
        P("track", "head"),
        P("track", "head"),
        P(),
        P("track", "head", None, None),
        P("track", "head", None, None),
    )
    out_specs = (P("head", "track", None), P(None, "track", "head"))
    return jax.shard_map(
        functools.partial(per_device, mesh.shape["head"], mesh.shape["track"]),
        mesh=mesh,
        in_specs=in_specs,
        out_specs=out_specs,
        check_vma=False,
    )
```

time: 1090 us -> 67.1 us (0.06)
  waiting for transfers between devices: 913 us -> 0 us
  local copies, waits for them, and re-layouts: 70.5 us -> 12.1 us
  Pallas kernels: 0 us -> 54 us
  starting transfers between devices: 36.8 us -> 0 us
  other arithmetic: 28.2 us -> 0 us
  matrix products: 23.2 us -> 0 us
  between operations: 14.5 us -> 0.66 us
    all_gather x1 -> x0, waiting for transfers between devices: 904 us -> none  [per_device(): table = lax.all_gather(surface, 'track', axis=1, tiled=True)]
    gather x2 -> x0, local copies, waits for them, and re-layouts: 62 us -> none  [per_device(): applied = jnp.take(table, cells, axis=1)]
    pallas_call x0 -> x1, Pallas kernels: none -> 54 us  [per_device(): pl.pallas_call(functools.partial(kernel, n_head, n_track), out_shape=(jax...]
    ppermute x12 -> x0, starting transfers between devices: 36.8 us -> none  [the longest x6 26 us: extended(): lax.ppermute(lax.slice_in_dim(block, block.shape[dim] - width, None, axis...]
    add x3 -> x0, other arithmetic: 27.5 us -> none  [the longest x2 26.7 us: relax_sweep(): return center + 0.8 * numer / denom]
    dot_general x8 -> x0, matrix products: 23.2 us -> none  [the longest x2 8.37 us: per_device(): ex = jnp.einsum('kij,ckj->cki', couple_self, tiles[:, 1:-1], precision=HIGH)]
  transfers between devices with their start and end apart: 13 -> 0, of which waited for: 7 -> 0; matrix products, arithmetic and copies ran while one was open for 1% -> 0% of each run, Pallas kernels for 0% -> 0%
where the time goes in v1:
time: 67.1 us; the launch traced here: 66.7 us
  Pallas kernels  54 us (80%)
  local copies, waits for them, and re-layouts  12.1 us (18%)
    pallas_call x1, Pallas kernels, per_device(): pl.pallas_call(functools.partial(kernel, n_head, n_track), out_shape=(jax...  54 us
    unnamed x16, local copies, waits for them, and re-layouts  12.1 us

profile of v1, /device:TPU:1, one launch (start us, length us, event | category | flops | bytes accessed | tf_op | source)
XLA Modules:
  0.0 66.7 jit_solution(3665872547883354541)
XLA Ops:
  0.6 0.0 copy-start
  0.6 1.6 %copy-done = f32[1,32,128,128]{3,2,1,0:T(8,128)S(1)} copy-done((f32[1,32,128,128]{3,2,1,0:T(8,128)S(1)}, f32[1,32,128,128]{3,2,1,0:T(8,128)}, u32[]{:S(2)}) %copy-start) | copy-done | bytes 2097176
  2.2 0.0 copy-start.1
  2.2 1.6 %copy-done.1 = f32[1,32,128,128]{3,2,1,0:T(8,128)S(1)} copy-done((f32[1,32,128,128]{3,2,1,0:T(8,128)S(1)}, f32[1,32,128,128]{3,2,1,0:T(8,128)}, u32[]{:S(2)}) %copy-start.1) | copy-done | bytes 2097176
  3.8 0.0 copy-start.2
  3.8 0.8 %copy-done.2 = f32[3,1,4096]{2,1,0:T(1,128)S(1)} copy-done((f32[3,1,4096]{2,1,0:T(1,128)S(1)}, f32[3,1,4096]{2,1,0:T(1,128)}, u32[]{:S(2)}) %copy-start.2) | copy-done | bytes 49176
  4.6 0.0 copy-start.3
  4.6 0.7 %copy-done.3 = s32[1,4096]{1,0:T(1,128)S(1)} copy-done((s32[1,4096]{1,0:T(1,128)S(1)}, s32[1,4096]{1,0:T(1,128)}, u32[]{:S(2)}) %copy-start.3) | copy-done | bytes 16408
  5.3 0.0 copy-start.4
  5.3 0.7 %copy-done.4 = s32[1,4096]{1,0:T(1,128)S(1)} copy-done((s32[1,4096]{1,0:T(1,128)S(1)}, s32[1,4096]{1,0:T(1,128)}, u32[]{:S(2)}) %copy-start.4) | copy-done | bytes 16408
  6.1 0.0 copy-start.5
  6.1 0.7 %copy-done.5 = f32[3,128]{1,0:T(4,128)S(1)} copy-done((f32[3,128]{1,0:T(4,128)S(1)}, f32[3,128]{1,0:T(4,128)}, u32[]{:S(2)}) %copy-start.5) | copy-done | bytes 1560
  6.7 0.0 copy-start.6
  6.7 0.7 copy-done.6
  7.4 54.0 %pole_and_grains.1 = (f32[64,128,128]{2,1,0:T(8,128)}, f32[3,32,128]{2,1,0:T(8,128)S(1)}) custom-call(f32[64,128,128]{2,1,0:T(8,128)} %pot_hbm.1, f32[64,128,128]{2,1,0:T(8,128)} %src_hbm.1, f32[3,128]{1,0:T(4,128)S(1)} %copy-done.5, f32[3,32,128]{2,1,0:T(8,128)S(1)} %bitcast.9, s32[32,128]{1,0:T(8,128)S(1)} %bitcast.11, s32[32,128]{1,0:T(8,128)S(1)} %bitcast.12, ...), custom_call_target="tpu_custom_call" | custom-call | tf_op jit(solution)/shard_map/pole_and_grains/pallas_call | solution.py:512
  61.4 4.7 %copy.15 = f32[64,128,128]{2,1,0:T(8,128)} copy(f32[64,128,128]{2,1,0:T(8,128)} %get-tuple-element.12) | data formatting | bytes 8388608
  66.1 0.6 copy.16
Async XLA Ops:
  0.6 1.6 %copy-start = (f32[1,32,128,128]{3,2,1,0:T(8,128)S(1)}, f32[1,32,128,128]{3,2,1,0:T(8,128)}, u32[]{:S(2)}) copy-start(f32[1,32,128,128]{3,2,1,0:T(8,128)} %param.16) | copy-start | bytes 6291460
  2.2 1.6 %copy-start.1 = (f32[1,32,128,128]{3,2,1,0:T(8,128)S(1)}, f32[1,32,128,128]{3,2,1,0:T(8,128)}, u32[]{:S(2)}) copy-start(f32[1,32,128,128]{3,2,1,0:T(8,128)} %param.17) | copy-start | bytes 6291460
  3.8 0.8 %copy-start.2 = (f32[3,1,4096]{2,1,0:T(1,128)S(1)}, f32[3,1,4096]{2,1,0:T(1,128)}, u32[]{:S(2)}) copy-start(f32[3,1,4096]{2,1,0:T(1,128)} %param.12) | copy-start | bytes 147460
  4.6 0.7 %copy-start.3 = (s32[1,4096]{1,0:T(1,128)S(1)}, s32[1,4096]{1,0:T(1,128)}, u32[]{:S(2)}) copy-start(s32[1,4096]{1,0:T(1,128)} %param.13) | copy-start | bytes 49156
  5.3 0.7 %copy-start.4 = (s32[1,4096]{1,0:T(1,128)S(1)}, s32[1,4096]{1,0:T(1,128)}, u32[]{:S(2)}) copy-start(s32[1,4096]{1,0:T(1,128)} %param.14) | copy-start | bytes 49156
  6.1 0.7 %copy-start.5 = (f32[3,128]{1,0:T(4,128)S(1)}, f32[3,128]{1,0:T(4,128)}, u32[]{:S(2)}) copy-start(f32[3,128]{1,0:T(4,128)} %dk_hbm.1) | copy-start | bytes 4612
  6.7 0.7 copy-start.6

commit v2 on v0

v2 whole, which is shorter than its diff:
```python
import functools

import jax
import jax.numpy as jnp
from jax import lax
from jax.experimental import pallas as pl
from jax.experimental.pallas import tpu as pltpu
from jax.sharding import PartitionSpec as P

F32 = jnp.float32
BF16 = jnp.bfloat16
I32 = jnp.int32
NN = (((1,), (0,)), ((), ()))
NT = (((1,), (1,)), ((), ()))
ROW0 = 8


def mxu(a, b, dims):
    return lax.dot_general(a, b, dims, preferred_element_type=F32)


def split(a):
    high = a.astype(BF16)
    return high, (a - high.astype(F32)).astype(BF16)


def face(a, b):
    differ = b - a
    perm = 1.0 + pltpu.reciprocal(0.25 + differ * differ)
    return perm, perm * differ


def relax_rows(center, upper, before, after, drive, carried, first, last):
    perm, flux = face(center, upper)
    numer = (drive - carried[1]) + flux
    denom = (1.0 + carried[0]) + perm
    carried = (perm, flux)
    perm, flux = face(before, center)
    numer = numer - flux
    denom = denom + perm
    depth = center.shape[1]
    for other in (
        after,
        jnp.where(last, 0.0, pltpu.roll(center, depth - 1, 1)),
        jnp.where(first, 0.0, pltpu.roll(center, 1, 1)),
    ):
        perm, flux = face(center, other)
        numer = numer + flux
        denom = denom + perm
    return center + (0.8 * numer) * pltpu.reciprocal(denom), carried


def one_hot_rows(index, count):
    lanes = index.shape[1]
    rows = lax.broadcasted_iota(I32, (count, lanes), 0)
    return jnp.where(rows == jnp.broadcast_to(index, (count, lanes)), 1.0, 0.0)


def lookup(table, address):
    hot = jnp.concatenate([one_hot_rows(a & 127, 128) for a in address], axis=1).astype(BF16)
    found = mxu(table, jnp.concatenate([hot, hot], axis=0), NN)
    results = []
    for part, a in enumerate(address):
        group = jnp.broadcast_to(a >> 8, (8, 128))
        odd = jnp.broadcast_to((a >> 7) & 1, (8, 128))
        total = jnp.zeros((8, 128), F32)
        for g in range(table.shape[0] // 8):
            total = total + jnp.where(
                group == g, found[8 * g : 8 * g + 8, 128 * part : 128 * part + 128], 0.0
            )
        results.append(jnp.where(odd == 0, total, pltpu.roll(total, 7, 0)))
    return results


def halves(rows):
    high, low = split(rows)
    return jnp.concatenate([high, low], axis=1)


def llb_section(state, field, target):
    mx, my, mz = state
    sq_norm = mx * mx + my * my + mz * mz
    pull = 0.5 * (1.0 - sq_norm / target)
    hx, hy, hz = (f + pull * m for f, m in zip(field, state))
    tx, ty, tz = my * hz - mz * hy, mz * hx - mx * hz, mx * hy - my * hx
    dx, dy, dz = my * tz - mz * ty, mz * tx - mx * tz, mx * ty - my * tx
    along = 0.3 * (mx * hx + my * hy + mz * hz)
    return tuple(
        m + 0.1 * (along * m - t - 0.5 * d)
        for m, t, d in zip(state, (tx, ty, tz), (dx, dy, dz))
    )


def has_neighbours(n_head, n_track):
    head = lax.axis_index("head")
    track = lax.axis_index("track")
    return head, track, head > 0, head < n_head - 1, track > 0, track < n_track - 1


def remote(a, b, send, recv, device):
    return pltpu.make_async_remote_copy(
        src_ref=a, dst_ref=b, send_sem=send, recv_sem=recv, device_id=device,
        device_id_type=pl.DeviceIdType.MESH,
    )


def start(copies):
    for there, copy in copies:

        @pl.when(there)
        def _():
            copy.start()


def finish(copies):
    for there, copy in copies:

        @pl.when(there)
        def _():
            copy.wait_send()
            copy.wait_recv()


def greet(n_head, n_track):
    head, track, has_low_x, has_high_x, _, _ = has_neighbours(n_head, n_track)
    barrier = pltpu.get_barrier_semaphore()

    def hello(step, _):
        other = (head, lax.rem(track + step, n_track))
        pl.semaphore_signal(barrier, inc=1, device_id=other, device_id_type=pl.DeviceIdType.MESH)
        return 0

    lax.fori_loop(1, n_track, hello, 0)
    for there, other in ((has_low_x, head - 1), (has_high_x, head + 1)):

        @pl.when(there)
        def _():
            pl.semaphore_signal(
                barrier, inc=1, device_id=(other, track), device_id_type=pl.DeviceIdType.MESH
            )

    return barrier, n_track - 1 + has_low_x.astype(I32) + has_high_x.astype(I32)


def rim_copies(n_head, n_track, source, target, send, recv, waits):
    head, track, has_low_x, has_high_x, _, _ = has_neighbours(n_head, n_track)
    low, high = (head - 1, track), (head + 1, track)
    if waits:
        return [
            (has_low_x, remote(source.at[0], target.at[0], send.at[0], recv.at[0], low)),
            (has_high_x, remote(source.at[1], target.at[1], send.at[1], recv.at[1], high)),
        ]
    return [
        (has_low_x, remote(source.at[0], target.at[1], send.at[0], recv.at[1], low)),
        (has_high_x, remote(source.at[1], target.at[0], send.at[1], recv.at[0], high)),
    ]


def put_edges(edge, state):
    edge[...] = jnp.zeros(edge.shape, F32)
    for comp, value in enumerate(state):
        last = value.shape[0] - 1
        edge[0, comp : comp + 1, :] = value[0:1, :]
        edge[1, comp : comp + 1, :] = value[last : last + 1, :]


def rank_grains(foot, addr, ask, n_track):
    later = lax.broadcasted_iota(I32, (128, 128), 0) < lax.broadcasted_iota(I32, (128, 128), 1)
    count_matrix = jnp.concatenate(
        [jnp.where(later, 1.0, 0.0), jnp.ones((128, 128), F32)], axis=1
    ).astype(BF16)
    before = jnp.zeros((n_track, 128), F32)
    asks = jnp.zeros((128, 128), F32)
    for chunk in range(foot.shape[0]):
        cell = foot[chunk : chunk + 1, :]
        owner = cell >> 13
        hot = one_hot_rows(owner, n_track)
        counts = mxu(hot.astype(BF16), count_matrix, NN)
        place = jnp.sum(hot * (counts[:, :128] + before), axis=0, keepdims=True).astype(I32)
        before = before + counts[:, 128:]
        where_at = owner * 256 + place
        addr[chunk : chunk + 1, :] = where_at
        row = one_hot_rows(where_at >> 7, 2 * n_track)
        lane = one_hot_rows(where_at & 127, 128)
        high = jnp.broadcast_to((cell >> 7) & 63, row.shape).astype(F32)
        low = jnp.broadcast_to(cell & 127, row.shape).astype(F32)
        values = jnp.concatenate([row * high, row * low], axis=0)
        asks = asks + mxu(values.astype(BF16), lane.astype(BF16), NT)
    ask[...] = jnp.zeros(ask.shape, I32)
    cells = (asks[: 2 * n_track] * 128.0 + asks[2 * n_track :]).astype(I32)
    for owner in range(n_track):
        ask[owner, 0:2, :] = cells[2 * owner : 2 * owner + 2, :]


def swept(source, src, x, row, rows_at, carried):
    lanes = lax.broadcasted_iota(I32, (rows_at, 128), 1)
    o = ROW0 + row
    rows = slice(o, o + rows_at)
    return relax_rows(
        source[x + 1, rows, :],
        source[x + 2, rows, :],
        source[x + 1, o - 1 : o - 1 + rows_at, :],
        source[x + 1, o + 1 : o + 1 + rows_at, :],
        src[x, row : row + rows_at, :],
        carried,
        lanes == 0,
        lanes == 127,
    )


def first_kernel(
    n_head, n_track,
    pot_hbm, src_hbm, mag_hbm, foot_hbm,
    mid, src, asked, addr, rim,
    pot, mag, foot, ask, edge,
    in_sem, halo_send, halo_recv, mid_send, mid_recv, rim_send, rim_recv, ask_send, ask_recv,
):
    head, track, has_low_x, has_high_x, has_low_y, has_high_y = has_neighbours(n_head, n_track)
    n_x, n_y, n_z = src.shape
    inner, all_x = pl.ds(ROW0, n_y), pl.ds(1, n_x)
    low_x, high_x = (head - 1, track), (head + 1, track)
    low_y, high_y = (head, track - 1), (head, track + 1)

    pairs = [
        (foot_hbm, foot),
        (mag_hbm, mag),
        (pot_hbm, pot.at[all_x, inner, :]),
        (src_hbm, src),
    ]
    loads = [pltpu.make_async_copy(a, b, in_sem.at[i]) for i, (a, b) in enumerate(pairs)]
    for copy in loads:
        copy.start()

    for ref in (pot, mid):
        for plane in (0, n_x + 1):
            ref[plane, ROW0 : ROW0 + n_y, :] = jnp.zeros((n_y, n_z), F32)
        for row in (ROW0 - 1, ROW0 + n_y):
            ref[1 : n_x + 1, row : row + 1, :] = jnp.zeros((n_x, 1, n_z), F32)
    rim[...] = jnp.zeros(rim.shape, F32)
    barrier, n_greeted = greet(n_head, n_track)
    loads[1].wait()
    put_edges(edge, [mag[comp] for comp in range(3)])
    pl.semaphore_wait(barrier, n_greeted)

    def halo(source, plane, row, target, send, recv):
        rows, planes = pl.ds(row, n_y), pl.ds(plane, n_x)
        return [
            (has_low_x, remote(source.at[plane, rows, :], target.at[n_x + 1, inner, :], send.at[0], recv.at[1], low_x)),
            (has_high_x, remote(source.at[plane + n_x - 1, rows, :], target.at[0, inner, :], send.at[1], recv.at[0], high_x)),
            (has_low_y, remote(source.at[planes, pl.ds(row, 1), :], target.at[all_x, pl.ds(ROW0 + n_y, 1), :], send.at[2], recv.at[3], low_y)),
            (has_high_y, remote(source.at[planes, pl.ds(row + n_y - 1, 1), :], target.at[all_x, pl.ds(ROW0 - 1, 1), :], send.at[3], recv.at[2], high_y)),
        ]

    def halo_waits(source, plane, row, target, send, recv):
        rows, planes = pl.ds(row, n_y), pl.ds(plane, n_x)
        return [
            (has_low_x, remote(source.at[plane, rows, :], target.at[0, inner, :], send.at[0], recv.at[0], low_x)),
            (has_high_x, remote(source.at[plane + n_x - 1, rows, :], target.at[n_x + 1, inner, :], send.at[1], recv.at[1], high_x)),
            (has_low_y, remote(source.at[planes, pl.ds(row, 1), :], target.at[all_x, pl.ds(ROW0 - 1, 1), :], send.at[2], recv.at[2], low_y)),
            (has_high_y, remote(source.at[planes, pl.ds(row + n_y - 1, 1), :], target.at[all_x, pl.ds(ROW0 + n_y, 1), :], send.at[3], recv.at[3], high_y)),
        ]

    start(halo(pot_hbm, 0, 0, pot, halo_send, halo_recv))
    start(rim_copies(n_head, n_track, edge, rim, rim_send, rim_recv, False))

    loads[0].wait()
    rank_grains(foot, addr, ask, n_track)
    asked[track] = ask[track]

    def send_ask(step, _):
        other = lax.rem(track + step, n_track)
        remote(ask.at[other], asked.at[track], ask_send.at[other], ask_recv.at[track], (head, other)).start()
        return 0

    lax.fori_loop(1, n_track, send_ask, 0)

    loads[2].wait()
    loads[3].wait()
    finish(halo_waits(pot_hbm, 0, 0, pot, halo_send, halo_recv))
    rows_at = 32
    chunks = range(0, n_y, rows_at)
    for x in (0, n_x - 1):
        for row in chunks:
            rows = slice(ROW0 + row, ROW0 + row + rows_at)
            mid[x + 1, rows, :], _ = swept(pot, src, x, row, rows_at, face(pot[x, rows, :], pot[x + 1, rows, :]))
    outer = halo(mid, 1, ROW0, mid, mid_send, mid_recv)
    start(outer[:2])
    unroll = 8
    for row in [chunks[0], chunks[-1], *chunks[1:-1]]:
        rows = slice(ROW0 + row, ROW0 + row + rows_at)

        def planes(base, count, carried):
            for j in range(count):
                mid[base + j + 1, rows, :], carried = swept(pot, src, base + j, row, rows_at, carried)
            return carried

        carried = face(pot[1, rows, :], pot[2, rows, :])
        trips = (n_x - 2) // unroll
        carried = lax.fori_loop(0, trips, lambda i, c: planes(1 + unroll * i, unroll, c), carried)
        planes(1 + unroll * trips, n_x - 2 - unroll * trips, carried)
        if row == chunks[-1]:
            start(outer[2:])

    def wait_ask(step, _):
        other = lax.rem(track + step, n_track)
        copy = remote(ask.at[other], asked.at[other], ask_send.at[other], ask_recv.at[other], (head, other))
        copy.wait_send()
        copy.wait_recv()
        return 0

    lax.fori_loop(1, n_track, wait_ask, 0)
    finish(rim_copies(n_head, n_track, edge, rim, rim_send, rim_recv, True))
    finish(halo_waits(mid, 1, ROW0, mid, mid_send, mid_recv))


def second_kernel(mid, src, asked, dk_hbm, out_hbm, answer, relaxed, dk, surf, carry, in_sem, out_sem):
    n_x, n_y, n_z = src.shape
    load = pltpu.make_async_copy(dk_hbm, dk, in_sem)
    load.start()
    load.wait()
    rows8 = lax.broadcasted_iota(I32, (8, 128), 0)
    kernels = []
    for odd in range(2):
        weights = jnp.zeros((8, 128), F32)
        for comp in range(3):
            weights = weights + jnp.where(
                rows8 == 2 * comp + odd, jnp.broadcast_to(dk[comp : comp + 1, :], (8, 128)), 0.0
            )
        high = weights.astype(BF16).astype(F32)
        kernels.append(jnp.concatenate([high, weights - high], axis=0))
    kernels = jnp.concatenate(kernels, axis=0).astype(BF16)
    kernels = jnp.concatenate([kernels, kernels], axis=1)

    rows_at = 32
    for row in range(0, n_y, rows_at):
        carry[0, row : row + rows_at, :], carry[1, row : row + rows_at, :] = face(
            mid[0, ROW0 + row : ROW0 + row + rows_at, :], mid[1, ROW0 + row : ROW0 + row + rows_at, :]
        )

    def pair(i, _):
        both = []
        for row in range(0, n_y, rows_at):
            here = slice(row, row + rows_at)
            carried = carry[0, here, :], carry[1, here, :]
            for odd in range(2):
                value, carried = swept(mid, src, 2 * i + odd, row, rows_at, carried)
                relaxed[2 * i + odd, here, :] = value
            carry[0, here, :], carry[1, here, :] = carried
        for odd in range(2):
            both.append(halves(relaxed[2 * i + odd]))
        pltpu.make_async_copy(relaxed.at[pl.ds(2 * i, 2)], out_hbm.at[pl.ds(2 * i, 2)], out_sem).start()
        found = mxu(kernels, jnp.concatenate(both, axis=0), NT)
        total = (found[0:8, :n_y] + found[8:16, :n_y]) + (found[16:24, n_y:] + found[24:32, n_y:])
        surf[pl.ds(pl.multiple_of(8 * i, 8), 8), :] = total
        return 0

    lax.fori_loop(0, n_x // 2, pair, 0)
    table = halves(surf[...])

    def reply(other, _):
        low, high = lookup(table, [asked[other, 0:1, :], asked[other, 1:2, :]])
        answer[other] = jnp.where(rows8 % 2 == 0, low, pltpu.roll(high, 1, 0))
        return 0

    lax.fori_loop(0, answer.shape[0], reply, 0, unroll=4)
    pltpu.make_async_copy(relaxed, out_hbm, out_sem).wait()


def third_kernel(
    n_head, n_track,
    answer, addr, rim, mag_hbm, temp_hbm, prof_hbm, self_hbm, next_hbm,
    mout_hbm,
    answered, mag, tidx, prof, tself, tnext, near_high, near_low, above, lhs, ex, rim_new, edge,
    in_sem, out_sem, rim_send, rim_recv, ans_send, ans_recv,
):
    head, track, *_ = has_neighbours(n_head, n_track)
    n_tiles, width = mag.shape[1:]
    pairs = [(self_hbm, tself), (next_hbm, tnext), (mag_hbm, mag), (temp_hbm, tidx), (prof_hbm, prof)]
    loads = [pltpu.make_async_copy(a, b, in_sem.at[i]) for i, (a, b) in enumerate(pairs)]
    for copy in loads:
        copy.start()
    rim_new[...] = jnp.zeros(rim_new.shape, F32)
    barrier, n_greeted = greet(n_head, n_track)

    def set_lhs(tile, value, comp):
        high = value.astype(BF16).astype(F32)
        lhs[pl.ds(16 * tile + comp, value.shape[0], stride=16), :] = high
        lhs[pl.ds(16 * tile + 8 + comp, value.shape[0], stride=16), :] = value - high

    lhs[...] = jnp.zeros(lhs.shape, F32)
    for copy in loads:
        copy.wait()
    for side, tile in ((0, 0), (1, n_tiles + 1)):
        high = rim[side].astype(BF16).astype(F32)
        lhs[16 * tile : 16 * tile + 8, :] = high
        lhs[16 * tile + 8 : 16 * tile + 16, :] = rim[side] - high
    state = [mag[comp] for comp in range(3)]
    for comp in range(3):
        set_lhs(1, state[comp], comp)
    profile = jnp.broadcast_to(prof[...], (8, 128))
    temp = jnp.concatenate(
        [jnp.take_along_axis(profile, tidx[at : at + 8, :], axis=1) for at in range(0, n_tiles, 8)], axis=0
    )
    target = 0.05 + jnp.maximum(1.0 - temp, 0.0)

    pl.semaphore_wait(barrier, n_greeted)
    answered[track] = answer[track]

    def send_answer(step, _):
        other = lax.rem(track + step, n_track)
        remote(answer.at[other], answered.at[track], ans_send.at[other], ans_recv.at[track], (head, other)).start()
        return 0

    lax.fori_loop(1, n_track, send_answer, 0)

    def get_lhs(tile):
        return lhs[pl.ds(pl.multiple_of(16 * tile, 16), 16), :].astype(BF16)

    def fold(parts):
        return parts[:8] + parts[8:]

    def exchange(k):
        near = jnp.concatenate([get_lhs(k + 1), get_lhs(k)], axis=1)
        far = get_lhs(k + 2)
        parts = mxu(near, near_high[k], NT) + mxu(near, near_low[k], NT)
        parts = parts + mxu(jnp.concatenate([far, far], axis=1), above[k], NN)
        ex[pl.ds(pl.multiple_of(8 * k, 8), 8), :] = fold(parts)

    def first_exchange(k, _):
        self_high, self_low = split(tself[k])
        next_high, next_low = split(tnext[k])
        near_high[k] = jnp.concatenate([self_high, next_high], axis=1)
        near_low[k] = jnp.concatenate([self_low, next_low], axis=1)
        above[k] = jnp.concatenate([next_high, next_low], axis=0)
        exchange(k)
        return 0

    def next_exchange(k, _):
        exchange(k)
        return 0

    def get_ex(comp):
        return ex[pl.ds(comp, n_tiles, stride=8), :]

    lax.fori_loop(0, n_tiles, first_exchange, 0, unroll=4)

    def wait_answer(step, _):
        other = lax.rem(track + step, n_track)
        copy = remote(answer.at[other], answered.at[other], ans_send.at[other], ans_recv.at[other], (head, other))
        copy.wait_send()
        copy.wait_recv()
        return 0

    lax.fori_loop(1, n_track, wait_answer, 0)
    table = halves(answered[...].reshape(8 * n_track, 128))
    applied = [[] for _ in range(3)]
    for pair in range(n_tiles // 2):
        found = lookup(table, [addr[2 * pair + i : 2 * pair + i + 1, :] for i in range(2)])
        for value in found:
            for comp in range(3):
                applied[comp].append(value[2 * comp : 2 * comp + 1, :])
    applied = [jnp.concatenate(rows, axis=0) for rows in applied]

    state = llb_section(state, [a + get_ex(comp) for comp, a in enumerate(applied)], target)
    put_edges(edge, state)
    start(rim_copies(n_head, n_track, edge, rim_new, rim_send, rim_recv, False))

    lhs[0:16, :] = jnp.zeros((16, width), F32)
    lhs[16 * (n_tiles + 1) :, :] = jnp.zeros((16, width), F32)
    for comp in range(3):
        set_lhs(1, state[comp], comp)
    lax.fori_loop(0, n_tiles, next_exchange, 0, unroll=4)
    finish(rim_copies(n_head, n_track, edge, rim_new, rim_send, rim_recv, True))
    end = n_tiles - 1
    for side, tile in ((0, 0), (1, end)):
        high = rim_new[side].astype(BF16).astype(F32)
        both = jnp.concatenate([high, rim_new[side] - high], axis=0).astype(BF16)
        if side == 0:
            parts = mxu(both, near_high[tile][:, width:], NT) + mxu(both, near_low[tile][:, width:], NT)
        else:
            parts = mxu(jnp.concatenate([both, both], axis=1), above[tile], NN)
        ex[8 * tile : 8 * tile + 8, :] = ex[8 * tile : 8 * tile + 8, :] + fold(parts)
    state = llb_section(state, [a + get_ex(comp) for comp, a in enumerate(applied)], target)
    for comp in range(3):
        mag[comp] = state[comp]
    result = pltpu.make_async_copy(mag, mout_hbm, out_sem)
    result.start()
    result.wait()


def per_device(n_head, n_track, potential, source, depth_kernel, magnet, footprint, temp_index, temp_profile, self_tiles, next_tiles):
    n_x, n_y, n_z = potential.shape
    n_tiles, width = self_tiles.shape[1], self_tiles.shape[2]
    padded = (n_x + 2, n_y + 16, n_z)
    hbm, vmem, dma = pltpu.HBM, pltpu.VMEM, pltpu.SemaphoreType.DMA
    in_hbm = pl.BlockSpec(memory_space=hbm)
    in_vmem = pl.BlockSpec(memory_space=vmem)

    def stay(*arrays):
        return [pltpu.with_memory_space_constraint(a, hbm) for a in arrays]

    potential, source, depth_kernel, magnet_in, footprint, temp_index, temp_profile, self_tiles, next_tiles = stay(
        potential,
        source,
        depth_kernel,
        magnet.reshape(3, n_tiles, width),
        footprint.reshape(n_tiles, width),
        temp_index.reshape(n_tiles, width),
        temp_profile.reshape(1, -1),
        self_tiles[0],
        next_tiles[0],
    )
    listed = (n_track, 8, width)
    mid, src, asked, addr, rim = pl.pallas_call(
        functools.partial(first_kernel, n_head, n_track),
        out_shape=(
            vmem(padded, F32),
            vmem((n_x, n_y, n_z), F32),
            vmem(listed, I32),
            vmem((n_tiles, width), I32),
            vmem((2, 8, width), F32),
        ),
        in_specs=[in_hbm] * 4,
        out_specs=(in_vmem,) * 5,
        scratch_shapes=[
            vmem(padded, F32),
            vmem((3, n_tiles, width), F32),
            vmem((n_tiles, width), I32),
            vmem(listed, I32),
            vmem((2, 8, width), F32),
            dma((4,)),
            *[dma((4,))] * 4,
            *[dma((2,))] * 2,
            *[dma((n_track,))] * 2,
        ],
        compiler_params=pltpu.CompilerParams(
            collective_id=0, has_side_effects=True, vmem_limit_bytes=10 << 20
        ),
        name="first_sweep",
    )(potential, source, magnet_in, footprint)
    relaxed, answer = pl.pallas_call(
        second_kernel,
        out_shape=(hbm((n_x, n_y, n_z), F32), vmem(listed, F32)),
        in_specs=[in_vmem] * 3 + [in_hbm],
        out_specs=(in_hbm, in_vmem),
        scratch_shapes=[
            vmem((n_x, n_y, n_z), F32),
            vmem((3, n_z), F32),
            vmem((8 * (n_x // 2), n_y), F32),
            vmem((2, n_y, n_z), F32),
            dma,
            dma,
        ],
        compiler_params=pltpu.CompilerParams(vmem_limit_bytes=10 << 20),
        name="second_sweep",
    )(mid, src, asked, depth_kernel)
    magnet_out = pl.pallas_call(
        functools.partial(third_kernel, n_head, n_track),
        out_shape=hbm((3, n_tiles, width), F32),
        in_specs=[in_vmem] * 3 + [in_hbm] * 5,
        out_specs=in_hbm,
        scratch_shapes=[
            vmem(listed, F32),
            vmem((3, n_tiles, width), F32),
            vmem((n_tiles, width), I32),
            vmem((1, 128), F32),
            vmem((n_tiles, width, width), F32),
            vmem((n_tiles, width, width), F32),
            vmem((n_tiles, width, 2 * width), BF16),
            vmem((n_tiles, width, 2 * width), BF16),
            vmem((n_tiles, 2 * width, width), BF16),
            vmem((16 * (n_tiles + 2), width), F32),
            vmem((8 * n_tiles, width), F32),
            vmem((2, 8, width), F32),
            vmem((2, 8, width), F32),
            dma((5,)),
            dma,
            *[dma((2,))] * 2,
            *[dma((n_track,))] * 2,
        ],
        compiler_params=pltpu.CompilerParams(
            collective_id=1, has_side_effects=True, vmem_limit_bytes=16 << 20
        ),
        name="sections",
    )(answer, addr, rim, magnet_in, temp_index, temp_profile, self_tiles, next_tiles)
    return relaxed, magnet_out.reshape(magnet.shape)


def solution(mesh):
    in_specs = (
        P("head", "track", None),
        P("head", "track", None),
        P(),
        P(None, "track", "head"),
        P("track", "head"),
        P("track", "head"),
        P(),
        P("track", "head", None, None),
        P("track", "head", None, None),
    )
    out_specs = (P("head", "track", None), P(None, "track", "head"))
    return jax.shard_map(
        functools.partial(per_device, mesh.shape["head"], mesh.shape["track"]),
        mesh=mesh,
        in_specs=in_specs,
        out_specs=out_specs,
        check_vma=False,
    )
```

time: 1090 us -> 58 us (0.05)
  waiting for transfers between devices: 913 us -> 0 us
  local copies, waits for them, and re-layouts: 70.5 us -> 1.42 us
  Pallas kernels: 0 us -> 55.7 us
  starting transfers between devices: 36.8 us -> 0 us
  other arithmetic: 28.2 us -> 0 us
  matrix products: 23.2 us -> 0 us
  between operations: 14.5 us -> 0.65 us
    all_gather x1 -> x0, waiting for transfers between devices: 904 us -> none  [per_device(): table = lax.all_gather(surface, 'track', axis=1, tiled=True)]
    gather x2 -> x0, local copies, waits for them, and re-layouts: 62 us -> none  [per_device(): applied = jnp.take(table, cells, axis=1)]
    pallas_call x0 -> x3, Pallas kernels: none -> 55.7 us  [the longest x1 22.2 us: per_device(): pl.pallas_call(functools.partial(first_kernel, n_head, n_track), out_shap...]
    ppermute x12 -> x0, starting transfers between devices: 36.8 us -> none  [the longest x6 26 us: extended(): lax.ppermute(lax.slice_in_dim(block, block.shape[dim] - width, None, axis...]
    add x3 -> x0, other arithmetic: 27.5 us -> none  [the longest x2 26.7 us: relax_sweep(): return center + 0.8 * numer / denom]
    dot_general x8 -> x0, matrix products: 23.2 us -> none  [the longest x2 8.37 us: per_device(): ex = jnp.einsum('kij,ckj->cki', couple_self, tiles[:, 1:-1], precision=HIGH)]
  transfers between devices with their start and end apart: 13 -> 0, of which waited for: 7 -> 0; matrix products, arithmetic and copies ran while one was open for 1% -> 0% of each run, Pallas kernels for 0% -> 0%
where the time goes in v2:
time: 58 us; the launch traced here: 57.8 us
  Pallas kernels  55.7 us (96%)
  local copies, waits for them, and re-layouts  1.42 us (2%)
  between operations  0.65 us (1%)
    pallas_call x1, Pallas kernels, per_device(): pl.pallas_call(functools.partial(first_kernel, n_head, n_track), out_shap...  22.2 us
    pallas_call x1, Pallas kernels, per_device(): pl.pallas_call(functools.partial(third_kernel, n_head, n_track), out_shap...  18.5 us
    pallas_call x1, Pallas kernels, per_device(): pl.pallas_call(second_kernel, out_shape=(hbm((n_x, n_y, n_z), F32), vmem(...  15.1 us
    unnamed x1, local copies, waits for them, and re-layouts  1.42 us

profile of v2, /device:TPU:1, one launch (start us, length us, event | category | flops | bytes accessed | tf_op | source)
XLA Modules:
  0.0 57.8 jit_solution(5356048638237699298)
XLA Ops:
  0.6 22.2 %first_sweep.1 = (f32[66,144,128]{2,1,0:T(8,128)S(1)}, f32[64,128,128]{2,1,0:T(8,128)S(1)}, s32[32,8,128]{2,1,0:T(8,128)S(1)}, s32[32,128]{1,0:T(8,128)S(1)}, f32[2,8,128]{2,1,0:T(8,128)S(1)}) custom-call(f32[64,128,128]{2,1,0:T(8,128)} %pot_hbm.1, f32[64,128,128]{2,1,0:T(8,128)} %src_hbm.1, f32[3,32,128]{2,1,0:T(8,128)} %bitcast.9, s32[32,128]{1,0:T(8,128)} %bitcast.12), custom_call_target="tpu_custom_call" | custom-call | tf_op jit(solution)/shard_map/first_sweep/pallas_call | solution.py:514
  22.8 15.1 %second_sweep.1 = (f32[64,128,128]{2,1,0:T(8,128)}, f32[32,8,128]{2,1,0:T(8,128)S(1)}) custom-call(f32[66,144,128]{2,1,0:T(8,128)S(1)} %get-tuple-element.9.mid, f32[64,128,128]{2,1,0:T(8,128)S(1)} %get-tuple-element.10.src, s32[32,8,128]{2,1,0:T(8,128)S(1)} %get-tuple-element.11.asked, f32[3,128]{1,0:T(4,128)} %dk_hbm.1), custom_call_target="tpu_custom_call" | custom-call | tf_op jit(solution)/shard_map/second_sweep/pallas_call | solution.py:541
  37.9 18.5 %sections.1 = f32[3,32,128]{2,1,0:T(8,128)} custom-call(f32[32,8,128]{2,1,0:T(8,128)S(1)} %get-tuple-element.13.answer, s32[32,128]{1,0:T(8,128)S(1)} %get-tuple-element.14.addr, f32[2,8,128]{2,1,0:T(8,128)S(1)} %get-tuple-element.15.rim, f32[3,32,128]{2,1,0:T(8,128)} %bitcast.10, s32[32,128]{1,0:T(8,128)} %bitcast.13, f32[1,128]{1,0:T(1,128)} %bitcast.14, ...), custom_call_target="tpu_custom_call" | custom-call | tf_op jit(solution)/shard_map/sections/pallas_call | solution.py:557
  56.4 1.4 %copy.14 = f32[3,1,4096]{2,1,0:T(1,128)} copy(f32[3,1,4096]{2,1,0:T(1,128)} %bitcast.11) | data formatting | bytes 98304

commit v3 on v2

v3 whole, which is shorter than its diff:
```python
import functools

import jax
import jax.numpy as jnp
from jax import lax
from jax.experimental import pallas as pl
from jax.experimental.pallas import tpu as pltpu
from jax.sharding import PartitionSpec as P

F32 = jnp.float32
BF16 = jnp.bfloat16
I32 = jnp.int32
NN = (((1,), (0,)), ((), ()))
NT = (((1,), (1,)), ((), ()))
ROW0 = 8
EARLY = 16


def mxu(a, b, dims):
    return lax.dot_general(a, b, dims, preferred_element_type=F32)


def split(a):
    high = a.astype(BF16)
    return high, (a - high.astype(F32)).astype(BF16)


def face(a, b):
    differ = b - a
    perm = 1.0 + pltpu.reciprocal(0.25 + differ * differ)
    return perm, perm * differ


def relax_rows(center, upper, before, after, drive, carried, first, last):
    perm, flux = face(center, upper)
    numer = (drive - carried[1]) + flux
    denom = (1.0 + carried[0]) + perm
    carried = (perm, flux)
    perm, flux = face(before, center)
    numer = numer - flux
    denom = denom + perm
    depth = center.shape[1]
    for other in (
        after,
        jnp.where(last, 0.0, pltpu.roll(center, depth - 1, 1)),
        jnp.where(first, 0.0, pltpu.roll(center, 1, 1)),
    ):
        perm, flux = face(center, other)
        numer = numer + flux
        denom = denom + perm
    return center + (0.8 * numer) * pltpu.reciprocal(denom), carried


def one_hot_rows(index, count):
    lanes = index.shape[1]
    rows = lax.broadcasted_iota(I32, (count, lanes), 0)
    return jnp.where(rows == jnp.broadcast_to(index, (count, lanes)), 1.0, 0.0)


def lookup(table, address):
    hot = jnp.concatenate([one_hot_rows(a & 127, 128) for a in address], axis=1).astype(BF16)
    found = mxu(table, jnp.concatenate([hot, hot], axis=0), NN)
    results = []
    for part, a in enumerate(address):
        group = jnp.broadcast_to(a >> 8, (8, 128))
        odd = jnp.broadcast_to((a >> 7) & 1, (8, 128))
        total = jnp.zeros((8, 128), F32)
        for g in range(table.shape[0] // 8):
            total = total + jnp.where(
                group == g, found[8 * g : 8 * g + 8, 128 * part : 128 * part + 128], 0.0
            )
        results.append(jnp.where(odd == 0, total, pltpu.roll(total, 7, 0)))
    return results


def halves(rows):
    high, low = split(rows)
    return jnp.concatenate([high, low], axis=1)


def llb_section(state, field, target):
    mx, my, mz = state
    sq_norm = mx * mx + my * my + mz * mz
    pull = 0.5 * (1.0 - sq_norm / target)
    hx, hy, hz = (f + pull * m for f, m in zip(field, state))
    tx, ty, tz = my * hz - mz * hy, mz * hx - mx * hz, mx * hy - my * hx
    dx, dy, dz = my * tz - mz * ty, mz * tx - mx * tz, mx * ty - my * tx
    along = 0.3 * (mx * hx + my * hy + mz * hz)
    return tuple(
        m + 0.1 * (along * m - t - 0.5 * d)
        for m, t, d in zip(state, (tx, ty, tz), (dx, dy, dz))
    )


def has_neighbours(n_head, n_track):
    head = lax.axis_index("head")
    track = lax.axis_index("track")
    return head, track, head > 0, head < n_head - 1, track > 0, track < n_track - 1


def remote(a, b, send, recv, device):
    return pltpu.make_async_remote_copy(
        src_ref=a, dst_ref=b, send_sem=send, recv_sem=recv, device_id=device,
        device_id_type=pl.DeviceIdType.MESH,
    )


def start(copies):
    for there, copy in copies:

        @pl.when(there)
        def _():
            copy.start()


def finish(copies):
    for there, copy in copies:

        @pl.when(there)
        def _():
            copy.wait_send()
            copy.wait_recv()


def greet(n_head, n_track):
    head, track, has_low_x, has_high_x, _, _ = has_neighbours(n_head, n_track)
    barrier = pltpu.get_barrier_semaphore()

    def hello(step, _):
        other = (head, lax.rem(track + step, n_track))
        pl.semaphore_signal(barrier, inc=1, device_id=other, device_id_type=pl.DeviceIdType.MESH)
        return 0

    lax.fori_loop(1, n_track, hello, 0)
    for there, other in ((has_low_x, head - 1), (has_high_x, head + 1)):

        @pl.when(there)
        def _():
            pl.semaphore_signal(
                barrier, inc=1, device_id=(other, track), device_id_type=pl.DeviceIdType.MESH
            )

    return barrier, n_track - 1 + has_low_x.astype(I32) + has_high_x.astype(I32)


def rim_copies(n_head, n_track, source, target, send, recv, waits):
    head, track, has_low_x, has_high_x, _, _ = has_neighbours(n_head, n_track)
    low, high = (head - 1, track), (head + 1, track)
    if waits:
        return [
            (has_low_x, remote(source.at[0], target.at[0], send.at[0], recv.at[0], low)),
            (has_high_x, remote(source.at[1], target.at[1], send.at[1], recv.at[1], high)),
        ]
    return [
        (has_low_x, remote(source.at[0], target.at[1], send.at[0], recv.at[1], low)),
        (has_high_x, remote(source.at[1], target.at[0], send.at[1], recv.at[0], high)),
    ]


def put_edges(edge, state):
    edge[...] = jnp.zeros(edge.shape, F32)
    for comp, value in enumerate(state):
        last = value.shape[0] - 1
        edge[0, comp : comp + 1, :] = value[0:1, :]
        edge[1, comp : comp + 1, :] = value[last : last + 1, :]


def rank_grains(foot, addr, ask, n_track):
    later = lax.broadcasted_iota(I32, (128, 128), 0) < lax.broadcasted_iota(I32, (128, 128), 1)
    count_matrix = jnp.concatenate(
        [jnp.where(later, 1.0, 0.0), jnp.ones((128, 128), F32)], axis=1
    ).astype(BF16)
    before = jnp.zeros((n_track, 128), F32)
    asks = jnp.zeros((128, 128), F32)
    for chunk in range(foot.shape[0]):
        cell = foot[chunk : chunk + 1, :]
        owner = cell >> 13
        hot = one_hot_rows(owner, n_track)
        counts = mxu(hot.astype(BF16), count_matrix, NN)
        place = jnp.sum(hot * (counts[:, :128] + before), axis=0, keepdims=True).astype(I32)
        before = before + counts[:, 128:]
        where_at = owner * 256 + place
        addr[chunk : chunk + 1, :] = where_at
        row = one_hot_rows(where_at >> 7, 2 * n_track)
        lane = one_hot_rows(where_at & 127, 128)
        high = jnp.broadcast_to((cell >> 7) & 63, row.shape).astype(F32)
        low = jnp.broadcast_to(cell & 127, row.shape).astype(F32)
        values = jnp.concatenate([row * high, row * low], axis=0)
        asks = asks + mxu(values.astype(BF16), lane.astype(BF16), NT)
    cells = (asks[: 2 * n_track] * 128.0 + asks[2 * n_track :]).astype(I32)
    for owner in range(n_track):
        ask[owner, 0:2, :] = cells[2 * owner : 2 * owner + 2, :]


def swept(source, src, x, row, rows_at, carried):
    lanes = lax.broadcasted_iota(I32, (rows_at, 128), 1)
    o = ROW0 + row
    rows = slice(o, o + rows_at)
    return relax_rows(
        source[x + 1, rows, :],
        source[x + 2, rows, :],
        source[x + 1, o - 1 : o - 1 + rows_at, :],
        source[x + 1, o + 1 : o + 1 + rows_at, :],
        src[x, row : row + rows_at, :],
        carried,
        lanes == 0,
        lanes == 127,
    )


def fold(parts):
    return parts[:8] + parts[8:]


def exchange(k, lhs, near_high, near_low, above, ex):
    def get_lhs(tile):
        return lhs[pl.ds(pl.multiple_of(16 * tile, 16), 16), :].astype(BF16)

    near = jnp.concatenate([get_lhs(k + 1), get_lhs(k)], axis=1)
    far = get_lhs(k + 2)
    parts = mxu(near, near_high[k], NT) + mxu(near, near_low[k], NT)
    parts = parts + mxu(jnp.concatenate([far, far], axis=1), above[k], NN)
    ex[pl.ds(pl.multiple_of(8 * k, 8), 8), :] = fold(parts)


def get_ex(ex):
    return [ex[pl.ds(comp, ex.shape[0] // 8, stride=8), :] for comp in range(3)]


def main_kernel(
    n_head, n_track,
    pot_hbm, src_hbm, dk_hbm, mag_hbm, foot_hbm, temp_hbm, prof_hbm, self_hbm, next_hbm,
    pot, near_high, near_low, above, lhs, ex, rim_new, state_out, applied_out, target_out,
    mid, src, dk, mag, foot, tidx, prof, tself, tnext,
    rim, edge, edge_new, lines, lines_in, lines_mid, lines_mid_in,
    addr, ask, asked, surf, answer, answered,
    in_sem, halo_send, halo_recv, mid_send, mid_recv, rim_send, rim_recv,
    rim_new_send, rim_new_recv, ask_send, ask_recv, ans_send, ans_recv,
):
    head, track, has_low_x, has_high_x, has_low_y, has_high_y = has_neighbours(n_head, n_track)
    n_x, n_y, n_z = src.shape
    n_tiles, width = mag.shape[1:]
    inner, all_x = pl.ds(ROW0, n_y), pl.ds(1, n_x)
    low_x, high_x = (head - 1, track), (head + 1, track)
    low_y, high_y = (head, track - 1), (head, track + 1)
    rows8 = lax.broadcasted_iota(I32, (8, 128), 0)

    pairs = [
        (foot_hbm, foot),
        (mag_hbm, mag),
        (pot_hbm.at[:, pl.ds(0, 1), :], lines.at[0]),
        (pot_hbm.at[:, pl.ds(n_y - 1, 1), :], lines.at[1]),
        (pot_hbm, pot.at[all_x, inner, :]),
        (src_hbm, src),
        (dk_hbm, dk),
        (temp_hbm, tidx),
        (prof_hbm, prof),
        (self_hbm, tself),
        (next_hbm, tnext),
    ]
    loads = [pltpu.make_async_copy(a, b, in_sem.at[i]) for i, (a, b) in enumerate(pairs)]
    for copy in loads:
        copy.start()

    for ref in (pot, mid):
        for plane in (0, n_x + 1):
            ref[plane, ROW0 : ROW0 + n_y, :] = jnp.zeros((n_y, n_z), F32)
    lines_in[...] = jnp.zeros(lines_in.shape, F32)
    lines_mid_in[...] = jnp.zeros(lines_mid_in.shape, F32)
    rim[...] = jnp.zeros(rim.shape, F32)
    rim_new[...] = jnp.zeros(rim_new.shape, F32)
    barrier, n_greeted = greet(n_head, n_track)
    loads[0].wait()
    rank_grains(foot, addr, ask, n_track)
    asked[track] = ask[track]
    loads[1].wait()
    put_edges(edge, [mag[comp] for comp in range(3)])
    loads[2].wait()
    loads[3].wait()
    pl.semaphore_wait(barrier, n_greeted)

    def halo(planes, rows, target, rows_in, send, recv):
        return [
            (has_low_x, remote(planes[0], target.at[n_x + 1, inner, :], send.at[0], recv.at[1], low_x)),
            (has_high_x, remote(planes[1], target.at[0, inner, :], send.at[1], recv.at[0], high_x)),
            (has_low_y, remote(rows.at[0], rows_in.at[1], send.at[2], recv.at[3], low_y)),
            (has_high_y, remote(rows.at[1], rows_in.at[0], send.at[3], recv.at[2], high_y)),
        ]

    def halo_waits(planes, rows, target, rows_in, send, recv):
        return [
            (has_low_x, remote(planes[0], target.at[0, inner, :], send.at[0], recv.at[0], low_x)),
            (has_high_x, remote(planes[1], target.at[n_x + 1, inner, :], send.at[1], recv.at[1], high_x)),
            (has_low_y, remote(rows.at[0], rows_in.at[0], send.at[2], recv.at[2], low_y)),
            (has_high_y, remote(rows.at[1], rows_in.at[1], send.at[3], recv.at[3], high_y)),
        ]

    def place_lines(rows_in, target):
        target[1 : n_x + 1, ROW0 - 1 : ROW0, :] = rows_in[0]
        target[1 : n_x + 1, ROW0 + n_y : ROW0 + n_y + 1, :] = rows_in[1]

    start_halo = [pot_hbm.at[0], pot_hbm.at[n_x - 1]], lines, pot, lines_in, halo_send, halo_recv
    start(halo(*start_halo))

    def send_ask(step, _):
        other = lax.rem(track + step, n_track)
        remote(ask.at[other], asked.at[track], ask_send.at[other], ask_recv.at[track], (head, other)).start()
        return 0

    lax.fori_loop(1, n_track, send_ask, 0)
    start(rim_copies(n_head, n_track, edge, rim, rim_send, rim_recv, False))
    loads[4].wait()
    loads[5].wait()

    rows_at = 32
    chunks = list(range(0, n_y, rows_at))
    unroll = 8

    def chunk_rows(row):
        return slice(ROW0 + row, ROW0 + row + rows_at)

    def sweep_chunk(source, target, row):
        rows = chunk_rows(row)

        def planes(base, count, carried):
            for j in range(count):
                target[base + j + 1, rows, :], carried = swept(source, src, base + j, row, rows_at, carried)
            return carried

        carried = face(source[1, rows, :], source[2, rows, :])
        trips = (n_x - 2) // unroll
        carried = lax.fori_loop(0, trips, lambda i, c: planes(1 + unroll * i, unroll, c), carried)
        planes(1 + unroll * trips, n_x - 2 - unroll * trips, carried)

    def sweep_outer(source, target):
        for x in (0, n_x - 1):
            for row in chunks:
                rows = chunk_rows(row)
                carried = face(source[x, rows, :], source[x + 1, rows, :])
                target[x + 1, rows, :], _ = swept(source, src, x, row, rows_at, carried)

    for row in chunks[1:-1]:
        sweep_chunk(pot, mid, row)
    finish(halo_waits(*start_halo))
    place_lines(lines_in, pot)
    sweep_outer(pot, mid)
    mid_halo = [mid.at[1, inner, :], mid.at[n_x, inner, :]], lines_mid, mid, lines_mid_in, mid_send, mid_recv
    sends = halo(*mid_halo)
    start(sends[:2])
    for row in (chunks[0], chunks[-1]):
        sweep_chunk(pot, mid, row)
    lines_mid[0] = mid[1 : n_x + 1, ROW0 : ROW0 + 1, :]
    lines_mid[1] = mid[1 : n_x + 1, ROW0 + n_y - 1 : ROW0 + n_y, :]
    start(sends[2:])

    for row in chunks[1:-1]:
        sweep_chunk(mid, pot, row)
    finish(halo_waits(*mid_halo))
    place_lines(lines_mid_in, mid)
    sweep_outer(mid, pot)
    for row in (chunks[0], chunks[-1]):
        sweep_chunk(mid, pot, row)

    loads[6].wait()
    kernels = []
    for odd in range(2):
        weights = jnp.zeros((8, 128), F32)
        for comp in range(3):
            weights = weights + jnp.where(
                rows8 == 2 * comp + odd, jnp.broadcast_to(dk[comp : comp + 1, :], (8, 128)), 0.0
            )
        high = weights.astype(BF16).astype(F32)
        kernels.append(jnp.concatenate([high, weights - high], axis=0))
    kernels = jnp.concatenate(kernels, axis=0).astype(BF16)
    kernels = jnp.concatenate([kernels, kernels], axis=1)

    def surface(i, _):
        both = [halves(pot[2 * i + odd + 1, ROW0 : ROW0 + n_y, :]) for odd in range(2)]
        found = mxu(kernels, jnp.concatenate(both, axis=0), NT)
        total = (found[0:8, :n_y] + found[8:16, :n_y]) + (found[16:24, n_y:] + found[24:32, n_y:])
        surf[pl.ds(pl.multiple_of(8 * i, 8), 8), :] = total
        return 0

    lax.fori_loop(0, n_x // 2, surface, 0, unroll=8)

    def wait_ask(step, _):
        other = lax.rem(track + step, n_track)
        copy = remote(ask.at[other], asked.at[other], ask_send.at[other], ask_recv.at[other], (head, other))
        copy.wait_send()
        copy.wait_recv()
        return 0

    lax.fori_loop(1, n_track, wait_ask, 0)
    table = halves(surf[...])

    def reply(group, own):
        for j in range(4):
            step = 4 * group + j
            other = lax.rem(track + step, n_track)
            low, high = lookup(table, [asked[other, 0:1, :], asked[other, 1:2, :]])
            tile = jnp.where(rows8 % 2 == 0, low, pltpu.roll(high, 1, 0))
            if own and j == 0:
                answered[track] = tile
            else:
                answer[other] = tile
                remote(answer.at[other], answered.at[track], ans_send.at[other], ans_recv.at[track], (head, other)).start()
        return 0

    reply(0, True)
    lax.fori_loop(1, n_track // 4, lambda group, _: reply(group, False), 0)

    def set_lhs(tile, value, comp):
        high = value.astype(BF16).astype(F32)
        lhs[pl.ds(16 * tile + comp, value.shape[0], stride=16), :] = high
        lhs[pl.ds(16 * tile + 8 + comp, value.shape[0], stride=16), :] = value - high

    lhs[...] = jnp.zeros(lhs.shape, F32)
    finish(rim_copies(n_head, n_track, edge, rim, rim_send, rim_recv, True))
    for side, tile in ((0, 0), (1, n_tiles + 1)):
        high = rim[side].astype(BF16).astype(F32)
        lhs[16 * tile : 16 * tile + 8, :] = high
        lhs[16 * tile + 8 : 16 * tile + 16, :] = rim[side] - high
    state = [mag[comp] for comp in range(3)]
    for comp in range(3):
        set_lhs(1, state[comp], comp)
    for copy in loads[7:]:
        copy.wait()

    def first_exchange(k, _):
        self_high, self_low = split(tself[k])
        next_high, next_low = split(tnext[k])
        near_high[k] = jnp.concatenate([self_high, next_high], axis=1)
        near_low[k] = jnp.concatenate([self_low, next_low], axis=1)
        above[k] = jnp.concatenate([next_high, next_low], axis=0)
        exchange(k, lhs, near_high, near_low, above, ex)
        return 0

    def next_exchange(k, _):
        exchange(k, lhs, near_high, near_low, above, ex)
        return 0

    lax.fori_loop(0, n_tiles, first_exchange, 0, unroll=4)
    profile = jnp.broadcast_to(prof[...], (8, 128))
    temp = jnp.concatenate(
        [jnp.take_along_axis(profile, tidx[at : at + 8, :], axis=1) for at in range(0, n_tiles, 8)], axis=0
    )
    target = 0.05 + jnp.maximum(1.0 - temp, 0.0)

    def wait_answer(step, _):
        other = lax.rem(track + step, n_track)
        copy = remote(answer.at[other], answered.at[other], ans_send.at[other], ans_recv.at[other], (head, other))
        copy.wait_send()
        copy.wait_recv()
        return 0

    lax.fori_loop(1, n_track, wait_answer, 0)
    table = halves(answered[...].reshape(8 * n_track, 128))
    applied = [[] for _ in range(3)]
    for pair in range(n_tiles // 2):
        found = lookup(table, [addr[2 * pair + i : 2 * pair + i + 1, :] for i in range(2)])
        for value in found:
            for comp in range(3):
                applied[comp].append(value[2 * comp : 2 * comp + 1, :])
    applied = [jnp.concatenate(rows, axis=0) for rows in applied]

    state = llb_section(state, [a + e for a, e in zip(applied, get_ex(ex))], target)
    put_edges(edge_new, state)
    start(rim_copies(n_head, n_track, edge_new, rim_new, rim_new_send, rim_new_recv, False))
    for comp in range(3):
        state_out[comp] = state[comp]
        applied_out[comp] = applied[comp]
    target_out[...] = target

    lhs[0:16, :] = jnp.zeros((16, width), F32)
    lhs[16 * (n_tiles + 1) :, :] = jnp.zeros((16, width), F32)
    for comp in range(3):
        set_lhs(1, state[comp], comp)
    lax.fori_loop(0, EARLY, next_exchange, 0, unroll=4)
    finish(rim_copies(n_head, n_track, edge_new, rim_new, rim_new_send, rim_new_recv, True))


def last_kernel(
    pot, near_high, near_low, above, lhs, ex_early, rim_new, state_in, applied, target,
    relaxed_hbm, magnet_hbm,
    ex, state_out, sem,
):
    n_x, n_y, _ = relaxed_hbm.shape
    n_tiles, width = target.shape
    store = pltpu.make_async_copy(pot.at[pl.ds(1, n_x), pl.ds(ROW0, n_y), :], relaxed_hbm, sem.at[0])
    store.start()
    ex[0 : 8 * EARLY, :] = ex_early[0 : 8 * EARLY, :]

    def next_exchange(k, _):
        exchange(k, lhs, near_high, near_low, above, ex)
        return 0

    lax.fori_loop(EARLY, n_tiles, next_exchange, 0, unroll=4)
    for side, tile in ((0, 0), (1, n_tiles - 1)):
        high = rim_new[side].astype(BF16).astype(F32)
        both = jnp.concatenate([high, rim_new[side] - high], axis=0).astype(BF16)
        if side == 0:
            parts = mxu(both, near_high[tile][:, width:], NT) + mxu(both, near_low[tile][:, width:], NT)
        else:
            parts = mxu(jnp.concatenate([both, both], axis=1), above[tile], NN)
        ex[8 * tile : 8 * tile + 8, :] = ex[8 * tile : 8 * tile + 8, :] + fold(parts)
    state = [state_in[comp] for comp in range(3)]
    fields = [applied[comp] + e for comp, e in enumerate(get_ex(ex))]
    for comp, value in enumerate(llb_section(state, fields, target[...])):
        state_out[comp] = value
    copy = pltpu.make_async_copy(state_out, magnet_hbm, sem.at[1])
    copy.start()
    copy.wait()
    store.wait()


def per_device(n_head, n_track, potential, source, depth_kernel, magnet, footprint, temp_index, temp_profile, self_tiles, next_tiles):
    n_x, n_y, n_z = potential.shape
    n_tiles, width = self_tiles.shape[1], self_tiles.shape[2]
    padded = (n_x + 2, n_y + 16, n_z)
    hbm, vmem, dma = pltpu.HBM, pltpu.VMEM, pltpu.SemaphoreType.DMA
    in_hbm = pl.BlockSpec(memory_space=hbm)
    in_vmem = pl.BlockSpec(memory_space=vmem)
    arguments = (
        potential,
        source,
        depth_kernel,
        magnet.reshape(3, n_tiles, width),
        footprint.reshape(n_tiles, width),
        temp_index.reshape(n_tiles, width),
        temp_profile.reshape(1, -1),
        self_tiles[0],
        next_tiles[0],
    )
    arguments = [pltpu.with_memory_space_constraint(a, hbm) for a in arguments]
    grains = (3, n_tiles, width)
    shared = (
        vmem(padded, F32),
        vmem((n_tiles, width, 2 * width), BF16),
        vmem((n_tiles, width, 2 * width), BF16),
        vmem((n_tiles, 2 * width, width), BF16),
        vmem((16 * (n_tiles + 2), width), F32),
        vmem((8 * n_tiles, width), F32),
        vmem((2, 8, width), F32),
        vmem(grains, F32),
        vmem(grains, F32),
        vmem((n_tiles, width), F32),
    )
    results = pl.pallas_call(
        functools.partial(main_kernel, n_head, n_track),
        out_shape=shared,
        in_specs=[in_hbm] * 9,
        out_specs=(in_vmem,) * len(shared),
        scratch_shapes=[
            vmem(padded, F32),
            vmem((n_x, n_y, n_z), F32),
            vmem((3, n_z), F32),
            vmem(grains, F32),
            vmem((n_tiles, width), I32),
            vmem((n_tiles, width), I32),
            vmem((1, 128), F32),
            vmem((n_tiles, width, width), F32),
            vmem((n_tiles, width, width), F32),
            *[vmem((2, 8, width), F32)] * 3,
            *[vmem((2, n_x, 1, n_z), F32)] * 4,
            vmem((n_tiles, width), I32),
            vmem((n_track, 2, width), I32),
            vmem((n_track, 2, width), I32),
            vmem((8 * (n_x // 2), n_y), F32),
            vmem((n_track, 8, width), F32),
            vmem((n_track, 8, width), F32),
            dma((11,)),
            *[dma((4,))] * 4,
            *[dma((2,))] * 4,
            *[dma((n_track,))] * 4,
        ],
        compiler_params=pltpu.CompilerParams(
            collective_id=0, has_side_effects=True, vmem_limit_bytes=24 << 20
        ),
        name="pole_and_grains",
    )(*arguments)
    relaxed, magnet_out = pl.pallas_call(
        last_kernel,
        out_shape=(hbm(potential.shape, F32), hbm(grains, F32)),
        in_specs=[in_vmem] * len(shared),
        out_specs=(in_hbm, in_hbm),
        scratch_shapes=[vmem((8 * n_tiles, width), F32), vmem(grains, F32), dma((2,))],
        compiler_params=pltpu.CompilerParams(vmem_limit_bytes=4 << 20),
        name="results",
    )(*results)
    return relaxed, magnet_out.reshape(magnet.shape)


def solution(mesh):
    in_specs = (
        P("head", "track", None),
        P("head", "track", None),
        P(),
        P(None, "track", "head"),
        P("track", "head"),
        P("track", "head"),
        P(),
        P("track", "head", None, None),
        P("track", "head", None, None),
    )
    out_specs = (P("head", "track", None), P(None, "track", "head"))
    return jax.shard_map(
        functools.partial(per_device, mesh.shape["head"], mesh.shape["track"]),
        mesh=mesh,
        in_specs=in_specs,
        out_specs=out_specs,
        check_vma=False,
    )
```

time: 58 us -> 46.6 us (0.80)
  Pallas kernels: 55.7 us -> 45.8 us
  local copies, waits for them, and re-layouts: 1.42 us -> 0 us
    pallas_call x3 -> x2, Pallas kernels: 55.7 us -> 45.8 us  [the longest x1 43.8 us: per_device(): pl.pallas_call(functools.partial(main_kernel, n_head, n_track), out_shape...]
    unnamed x1 -> x0, local copies, waits for them, and re-layouts: 1.42 us -> none
where the time goes in v3:
time: 46.6 us; the launch traced here: 46.5 us
  Pallas kernels  45.8 us (98%)
  between operations  0.64 us (1%)
    pallas_call x1, Pallas kernels, per_device(): pl.pallas_call(functools.partial(main_kernel, n_head, n_track), out_shape...  43.8 us
    pallas_call x1, Pallas kernels, per_device(): pl.pallas_call(last_kernel, out_shape=(hbm(potential.shape, F32), hbm(gra...  2.04 us

profile of v3, /device:TPU:1, one launch (start us, length us, event | category | flops | bytes accessed | tf_op | source)
XLA Modules:
  0.0 46.5 jit_solution(3724240658776275413)
XLA Ops:
  0.6 43.8 %pole_and_grains.1 = (f32[66,144,128]{2,1,0:T(8,128)S(1)}, bf16[32,128,256]{2,1,0:T(8,128)(2,1)S(1)}, bf16[32,128,256]{2,1,0:T(8,128)(2,1)S(1)}, bf16[32,256,128...) custom-call(f32[64,128,128]{2,1,0:T(8,128)} %pot_hbm.1, ...), custom_call_target="tpu_custom_call" | custom-call | tf_op jit(solution)/shard_map/pole_and_grains/pallas_call | solution.py:548
  44.4 2.0 %results.1 = (f32[64,128,128]{2,1,0:T(8,128)}, f32[3,32,128]{2,1,0:T(8,128)}) custom-call(f32[66,144,128]{2,1,0:T(8,128)S(1)} %get-tuple-element.14.pot, bf16[32,128,256]{2,1,0:T(8,128)(2,1)S(1)} %get-tuple-element.15.near_high, bf16[32,128,256]{2,1,0:T(8,128)(2,1)S(1)} %get-tuple-element.16.near_low, bf16[32,256,128]{2,1,0:T(8,128)(2,1)S(1)} %get-tuple-element.17.above, ...), custom_call_target="tpu_custom_call" | custom-call | tf_op jit(solution)/shard_map/results/pallas_call | solution.py:581

commit v4 on v3

--- a/solution.py
+++ b/solution.py
@@ -29,26 +29,6 @@
     differ = b - a
     perm = 1.0 + pltpu.reciprocal(0.25 + differ * differ)
     return perm, perm * differ
-
-
-def relax_rows(center, upper, before, after, drive, carried, first, last):
-    perm, flux = face(center, upper)
-    numer = (drive - carried[1]) + flux
-    denom = (1.0 + carried[0]) + perm
-    carried = (perm, flux)
-    perm, flux = face(before, center)
-    numer = numer - flux
-    denom = denom + perm
-    depth = center.shape[1]
-    for other in (
-        after,
-        jnp.where(last, 0.0, pltpu.roll(center, depth - 1, 1)),
-        jnp.where(first, 0.0, pltpu.roll(center, 1, 1)),
-    ):
-        perm, flux = face(center, other)
-        numer = numer + flux
-        denom = denom + perm
-    return center + (0.8 * numer) * pltpu.reciprocal(denom), carried
 
 
 def one_hot_rows(index, count):
@@ -113,13 +93,15 @@
             copy.start()
 
 
-def finish(copies):
+def finish(copies, sent):
     for there, copy in copies:
 
         @pl.when(there)
         def _():
-            copy.wait_send()
-            copy.wait_recv()
+            if sent:
+                copy.wait_send()
+            else:
+                copy.wait_recv()
 
 
 def greet(n_head, n_track):
@@ -157,12 +139,13 @@
     ]
 
 
-def put_edges(edge, state):
+def put_edges(edge, sides):
     edge[...] = jnp.zeros(edge.shape, F32)
-    for comp, value in enumerate(state):
-        last = value.shape[0] - 1
-        edge[0, comp : comp + 1, :] = value[0:1, :]
-        edge[1, comp : comp + 1, :] = value[last : last + 1, :]
+    for comp in range(3):
+        low, high = sides[0][comp], sides[1][comp]
+        last = high.shape[0] - 1
+        edge[0, comp : comp + 1, :] = low[0:1, :]
+        edge[1, comp : comp + 1, :] = high[last : last + 1, :]
 
 
 def rank_grains(foot, addr, ask, n_track):
@@ -192,20 +175,34 @@
         ask[owner, 0:2, :] = cells[2 * owner : 2 * owner + 2, :]
 
 
-def swept(source, src, x, row, rows_at, carried):
+def swept(source, src, faces, slot, x, row, rows_at, carried):
     lanes = lax.broadcasted_iota(I32, (rows_at, 128), 1)
     o = ROW0 + row
-    rows = slice(o, o + rows_at)
-    return relax_rows(
-        source[x + 1, rows, :],
-        source[x + 2, rows, :],
-        source[x + 1, o - 1 : o - 1 + rows_at, :],
-        source[x + 1, o + 1 : o + 1 + rows_at, :],
-        src[x, row : row + rows_at, :],
-        carried,
-        lanes == 0,
-        lanes == 127,
-    )
+    center = source[x + 1, o : o + rows_at, :]
+    depth = center.shape[1]
+    perm, flux = face(center, source[x + 2, o : o + rows_at, :])
+    numer = (src[x, row : row + rows_at, :] - carried[1]) + flux
+    denom = (1.0 + carried[0]) + perm
+    carried = (perm, flux)
+    perm, flux = face(source[x + 1, o - 1 : o - 1 + rows_at, :], center)
+    faces[0, slot, 0:rows_at, :] = perm
+    faces[1, slot, 0:rows_at, :] = flux
+    numer = numer - flux
+    denom = denom + perm
+    end = o + rows_at
+    perm, flux = face(source[x + 1, end - 1 : end, :], source[x + 1, end : end + 1, :])
+    faces[0, slot, rows_at : rows_at + 1, :] = perm
+    faces[1, slot, rows_at : rows_at + 1, :] = flux
+    for other in (
+        jnp.where(lanes == depth - 1, 0.0, pltpu.roll(center, depth - 1, 1)),
+        jnp.where(lanes == 0, 0.0, pltpu.roll(center, 1, 1)),
+    ):
+        perm, flux = face(center, other)
+        numer = numer + flux
+        denom = denom + perm
+    numer = numer + faces[1, slot, 1 : rows_at + 1, :]
+    denom = denom + faces[0, slot, 1 : rows_at + 1, :]
+    return center + (0.8 * numer) * pltpu.reciprocal(denom), carried
 
 
 def fold(parts):
@@ -231,7 +228,7 @@
     n_head, n_track,
     pot_hbm, src_hbm, dk_hbm, mag_hbm, foot_hbm, temp_hbm, prof_hbm, self_hbm, next_hbm,
     pot, near_high, near_low, above, lhs, ex, rim_new, state_out, applied_out, target_out,
-    mid, src, dk, mag, foot, tidx, prof, tself, tnext,
+    mid, src, faces, dk, mag, foot, tidx, prof, tself, tnext,
     rim, edge, edge_new, lines, lines_in, lines_mid, lines_mid_in,
     addr, ask, asked, surf, answer, answered,
     in_sem, halo_send, halo_recv, mid_send, mid_recv, rim_send, rim_recv,
@@ -245,6 +242,7 @@
     low_y, high_y = (head, track - 1), (head, track + 1)
     rows8 = lax.broadcasted_iota(I32, (8, 128), 0)
 
+    barrier, n_greeted = greet(n_head, n_track)
     pairs = [
         (foot_hbm, foot),
         (mag_hbm, mag),
@@ -262,19 +260,27 @@
     for copy in loads:
         copy.start()
 
-    for ref in (pot, mid):
-        for plane in (0, n_x + 1):
-            ref[plane, ROW0 : ROW0 + n_y, :] = jnp.zeros((n_y, n_z), F32)
-    lines_in[...] = jnp.zeros(lines_in.shape, F32)
-    lines_mid_in[...] = jnp.zeros(lines_mid_in.shape, F32)
-    rim[...] = jnp.zeros(rim.shape, F32)
-    rim_new[...] = jnp.zeros(rim_new.shape, F32)
-    barrier, n_greeted = greet(n_head, n_track)
+    for side, there in enumerate((has_low_x, has_high_x)):
+
+        @pl.when(jnp.logical_not(there))
+        def _():
+            for ref in (pot, mid):
+                ref[side * (n_x + 1), ROW0 : ROW0 + n_y, :] = jnp.zeros((n_y, n_z), F32)
+            for ref in (rim, rim_new):
+                ref[side] = jnp.zeros(ref.shape[1:], F32)
+
+    for side, there in enumerate((has_low_y, has_high_y)):
+
+        @pl.when(jnp.logical_not(there))
+        def _():
+            for ref in (lines_in, lines_mid_in):
+                ref[side] = jnp.zeros(ref.shape[1:], F32)
+
     loads[0].wait()
     rank_grains(foot, addr, ask, n_track)
     asked[track] = ask[track]
     loads[1].wait()
-    put_edges(edge, [mag[comp] for comp in range(3)])
+    put_edges(edge, [[mag[comp] for comp in range(3)]] * 2)
     loads[2].wait()
     loads[3].wait()
     pl.semaphore_wait(barrier, n_greeted)
@@ -312,55 +318,56 @@
     loads[4].wait()
     loads[5].wait()
 
-    rows_at = 32
-    chunks = list(range(0, n_y, rows_at))
-    unroll = 8
-
-    def chunk_rows(row):
-        return slice(ROW0 + row, ROW0 + row + rows_at)
-
-    def sweep_chunk(source, target, row):
-        rows = chunk_rows(row)
+    edge_rows = 32
+
+    def sweep_chunk(source, target, row, rows_at, unroll, beside=None):
+        rows = slice(ROW0 + row, ROW0 + row + rows_at)
 
         def planes(base, count, carried):
             for j in range(count):
-                target[base + j + 1, rows, :], carried = swept(source, src, base + j, row, rows_at, carried)
+                target[base + j + 1, rows, :], carried = swept(source, src, faces, j, base + j, row, rows_at, carried)
             return carried
 
-        carried = face(source[1, rows, :], source[2, rows, :])
+        def trip(i, carried):
+            if beside is not None:
+                beside(i)
+            return planes(1 + unroll * i, unroll, carried)
+
         trips = (n_x - 2) // unroll
-        carried = lax.fori_loop(0, trips, lambda i, c: planes(1 + unroll * i, unroll, c), carried)
+        carried = planes(1, unroll, face(source[1, rows, :], source[2, rows, :]))
+        carried = lax.fori_loop(1, trips, trip, carried)
+        if beside is not None:
+            beside(trips)
         planes(1 + unroll * trips, n_x - 2 - unroll * trips, carried)
 
+    def sweep_inner(source, target):
+        sweep_chunk(source, target, edge_rows, n_y - 2 * edge_rows, 4)
+
     def sweep_outer(source, target):
-        for x in (0, n_x - 1):
-            for row in chunks:
-                rows = chunk_rows(row)
+        for side, x in enumerate((0, n_x - 1)):
+            for row in range(0, n_y, edge_rows):
+                rows = slice(ROW0 + row, ROW0 + row + edge_rows)
                 carried = face(source[x, rows, :], source[x + 1, rows, :])
-                target[x + 1, rows, :], _ = swept(source, src, x, row, rows_at, carried)
-
-    for row in chunks[1:-1]:
-        sweep_chunk(pot, mid, row)
-    finish(halo_waits(*start_halo))
+                slot = 4 * side + row // edge_rows
+                target[x + 1, rows, :], _ = swept(source, src, faces, slot, x, row, edge_rows, carried)
+
+    def sweep_edge(source, target, row, beside=None):
+        sweep_chunk(source, target, row, edge_rows, 8, beside)
+
+    sweep_inner(pot, mid)
+    finish(halo_waits(*start_halo), False)
     place_lines(lines_in, pot)
     sweep_outer(pot, mid)
     mid_halo = [mid.at[1, inner, :], mid.at[n_x, inner, :]], lines_mid, mid, lines_mid_in, mid_send, mid_recv
     sends = halo(*mid_halo)
     start(sends[:2])
-    for row in (chunks[0], chunks[-1]):
-        sweep_chunk(pot, mid, row)
+    for row in (0, n_y - edge_rows):
+        sweep_edge(pot, mid, row)
     lines_mid[0] = mid[1 : n_x + 1, ROW0 : ROW0 + 1, :]
     lines_mid[1] = mid[1 : n_x + 1, ROW0 + n_y - 1 : ROW0 + n_y, :]
     start(sends[2:])
 
-    for row in chunks[1:-1]:
-        sweep_chunk(mid, pot, row)
-    finish(halo_waits(*mid_halo))
-    place_lines(lines_mid_in, mid)
-    sweep_outer(mid, pot)
-    for row in (chunks[0], chunks[-1]):
-        sweep_chunk(mid, pot, row)
-
+    sweep_inner(mid, pot)
     loads[6].wait()
     kernels = []
     for odd in range(2):
@@ -374,40 +381,51 @@
     kernels = jnp.concatenate(kernels, axis=0).astype(BF16)
     kernels = jnp.concatenate([kernels, kernels], axis=1)
 
-    def surface(i, _):
-        both = [halves(pot[2 * i + odd + 1, ROW0 : ROW0 + n_y, :]) for odd in range(2)]
-        found = mxu(kernels, jnp.concatenate(both, axis=0), NT)
-        total = (found[0:8, :n_y] + found[8:16, :n_y]) + (found[16:24, n_y:] + found[24:32, n_y:])
-        surf[pl.ds(pl.multiple_of(8 * i, 8), 8), :] = total
-        return 0
-
-    lax.fori_loop(0, n_x // 2, surface, 0, unroll=8)
+    def surface(i):
+        for j in range(4):
+            at = 4 * (i - 1) + j
+            both = [halves(pot[2 * at + odd + 1, ROW0 : ROW0 + n_y, :]) for odd in range(2)]
+            found = mxu(kernels, jnp.concatenate(both, axis=0), NT)
+            total = (found[0:8, :n_y] + found[8:16, :n_y]) + (found[16:24, n_y:] + found[24:32, n_y:])
+            surf[pl.ds(8 * at if isinstance(at, int) else pl.multiple_of(8 * at, 8), 8), :] = total
+
+    finish(halo_waits(*mid_halo), False)
+    place_lines(lines_mid_in, mid)
+    sweep_outer(mid, pot)
+    sweep_edge(mid, pot, 0)
+    sweep_edge(mid, pot, n_y - edge_rows, surface)
+    surface(n_x // 8)
 
     def wait_ask(step, _):
         other = lax.rem(track + step, n_track)
-        copy = remote(ask.at[other], asked.at[other], ask_send.at[other], ask_recv.at[other], (head, other))
-        copy.wait_send()
-        copy.wait_recv()
+        remote(ask.at[other], asked.at[other], ask_send.at[other], ask_recv.at[other], (head, other)).wait_recv()
         return 0
 
     lax.fori_loop(1, n_track, wait_ask, 0)
     table = halves(surf[...])
 
-    def reply(group, own):
-        for j in range(4):
-            step = 4 * group + j
-            other = lax.rem(track + step, n_track)
+    def reply(far_y, own):
+        y, z, x = track // 8, (track // 4) % 2, track % 4
+        others = [
+            (y + far_y) % 4 * 8 + (z + far_z) % 2 * 4 + (x + far_x) % 4
+            for far_z in (1, 0)
+            for far_x in (2, 1, 3, 0)
+        ]
+        for other in others:
             low, high = lookup(table, [asked[other, 0:1, :], asked[other, 1:2, :]])
-            tile = jnp.where(rows8 % 2 == 0, low, pltpu.roll(high, 1, 0))
-            if own and j == 0:
-                answered[track] = tile
-            else:
-                answer[other] = tile
-                remote(answer.at[other], answered.at[track], ans_send.at[other], ans_recv.at[track], (head, other)).start()
-        return 0
-
+            answer[other] = jnp.where(rows8 % 2 == 0, low, pltpu.roll(high, 1, 0))
+        if own:
+            answered[track] = answer[track]
+            others = others[:-1]
+        for other in others:
+            remote(answer.at[other], answered.at[track], ans_send.at[other], ans_recv.at[track], (head, other)).start()
+
+    def reply_far(group, _):
+        reply(jnp.where(group == 0, 2, jnp.where(group == 1, 1, 3)), False)
+        return 0
+
+    lax.fori_loop(0, 3, reply_far, 0)
     reply(0, True)
-    lax.fori_loop(1, n_track // 4, lambda group, _: reply(group, False), 0)
 
     def set_lhs(tile, value, comp):
         high = value.astype(BF16).astype(F32)
@@ -415,7 +433,7 @@
         lhs[pl.ds(16 * tile + 8 + comp, value.shape[0], stride=16), :] = value - high
 
     lhs[...] = jnp.zeros(lhs.shape, F32)
-    finish(rim_copies(n_head, n_track, edge, rim, rim_send, rim_recv, True))
+    finish(rim_copies(n_head, n_track, edge, rim, rim_send, rim_recv, True), False)
     for side, tile in ((0, 0), (1, n_tiles + 1)):
         high = rim[side].astype(BF16).astype(F32)
         lhs[16 * tile : 16 * tile + 8, :] = high
@@ -448,24 +466,37 @@
 
     def wait_answer(step, _):
         other = lax.rem(track + step, n_track)
-        copy = remote(answer.at[other], answered.at[other], ans_send.at[other], ans_recv.at[other], (head, other))
-        copy.wait_send()
-        copy.wait_recv()
+        remote(answer.at[other], answered.at[other], ans_send.at[other], ans_recv.at[other], (head, other)).wait_recv()
         return 0
 
     lax.fori_loop(1, n_track, wait_answer, 0)
     table = halves(answered[...].reshape(8 * n_track, 128))
-    applied = [[] for _ in range(3)]
-    for pair in range(n_tiles // 2):
+    applied = [[None] * n_tiles for _ in range(3)]
+
+    def find(pair):
         found = lookup(table, [addr[2 * pair + i : 2 * pair + i + 1, :] for i in range(2)])
-        for value in found:
+        for i, value in enumerate(found):
             for comp in range(3):
-                applied[comp].append(value[2 * comp : 2 * comp + 1, :])
+                applied[comp][2 * pair + i] = value[2 * comp : 2 * comp + 1, :]
+
+    last_pair = n_tiles // 2 - 1
+    find(0)
+    find(last_pair)
+    exs = get_ex(ex)
+    blank = jnp.zeros((6, width), F32)
+    sides = []
+    for rows, order in ((slice(0, 8), (0, 1, None)), (slice(n_tiles - 8, n_tiles), (None, n_tiles - 2, n_tiles - 1))):
+        fields = [
+            jnp.concatenate([blank if at is None else applied[comp][at] for at in order], axis=0) + exs[comp][rows]
+            for comp in range(3)
+        ]
+        sides.append(llb_section([m[rows] for m in state], fields, target[rows]))
+    put_edges(edge_new, sides)
+    start(rim_copies(n_head, n_track, edge_new, rim_new, rim_new_send, rim_new_recv, False))
+    for pair in range(1, last_pair):
+        find(pair)
     applied = [jnp.concatenate(rows, axis=0) for rows in applied]
-
-    state = llb_section(state, [a + e for a, e in zip(applied, get_ex(ex))], target)
-    put_edges(edge_new, state)
-    start(rim_copies(n_head, n_track, edge_new, rim_new, rim_new_send, rim_new_recv, False))
+    state = llb_section(state, [a + e for a, e in zip(applied, exs)], target)
     for comp in range(3):
         state_out[comp] = state[comp]
         applied_out[comp] = applied[comp]
@@ -476,7 +507,20 @@
     for comp in range(3):
         set_lhs(1, state[comp], comp)
     lax.fori_loop(0, EARLY, next_exchange, 0, unroll=4)
-    finish(rim_copies(n_head, n_track, edge_new, rim_new, rim_new_send, rim_new_recv, True))
+
+    def wait_sent(step, _):
+        other = lax.rem(track + step, n_track)
+        remote(ask.at[other], asked.at[other], ask_send.at[other], ask_recv.at[other], (head, other)).wait_send()
+        remote(answer.at[other], answered.at[other], ans_send.at[other], ans_recv.at[other], (head, other)).wait_send()
+        return 0
+
+    lax.fori_loop(1, n_track, wait_sent, 0)
+    finish(halo_waits(*start_halo), True)
+    finish(halo_waits(*mid_halo), True)
+    finish(rim_copies(n_head, n_track, edge, rim, rim_send, rim_recv, True), True)
+    new_rim = rim_copies(n_head, n_track, edge_new, rim_new, rim_new_send, rim_new_recv, True)
+    finish(new_rim, True)
+    finish(new_rim, False)
 
 
 def last_kernel(
@@ -553,6 +597,7 @@
         scratch_shapes=[
             vmem(padded, F32),
             vmem((n_x, n_y, n_z), F32),
+            vmem((2, 8, n_y, n_z), F32),
             vmem((3, n_z), F32),
             vmem(grains, F32),
             vmem((n_tiles, width), I32),

time: 46.6 us -> 41.4 us (0.89)
  Pallas kernels: 45.8 us -> 40.6 us
    pallas_call x1, Pallas kernels: 43.8 us -> 38.5 us  [per_device(): pl.pallas_call(functools.partial(main_kernel, n_head, n_track), out_shape...]
where the time goes in v4:
time: 41.4 us; the launch traced here: 41.2 us
  Pallas kernels  40.6 us (98%)
  between operations  0.64 us (2%)
    pallas_call x1, Pallas kernels, per_device(): pl.pallas_call(functools.partial(main_kernel, n_head, n_track), out_shape...  38.5 us
    pallas_call x1, Pallas kernels, per_device(): pl.pallas_call(last_kernel, out_shape=(hbm(potential.shape, F32), hbm(gra...  2.04 us

profile of v4, /device:TPU:1, one launch (start us, length us, event | category | flops | bytes accessed | tf_op | source)
XLA Modules:
  0.0 41.2 jit_solution(13494024042233479958)
XLA Ops:
  0.6 38.5 %pole_and_grains.1 = (f32[66,144,128]{2,1,0:T(8,128)S(1)}, bf16[32,128,256]{2,1,0:T(8,128)(2,1)S(1)}, bf16[32,128,256]{2,1,0:T(8,128)(2,1)S(1)}, bf16[32,256,128...) custom-call(f32[64,128,128]{2,1,0:T(8,128)} %pot_hbm.1, ...), custom_call_target="tpu_custom_call" | custom-call | tf_op jit(solution)/shard_map/pole_and_grains/pallas_call | solution.py:592
  39.2 2.0 %results.1 = (f32[64,128,128]{2,1,0:T(8,128)}, f32[3,32,128]{2,1,0:T(8,128)}) custom-call(f32[66,144,128]{2,1,0:T(8,128)S(1)} %get-tuple-element.14.pot, bf16[32,128,256]{2,1,0:T(8,128)(2,1)S(1)} %get-tuple-element.15.near_high, bf16[32,128,256]{2,1,0:T(8,128)(2,1)S(1)} %get-tuple-element.16.near_low, bf16[32,256,128]{2,1,0:T(8,128)(2,1)S(1)} %get-tuple-element.17.above, ...), custom_call_target="tpu_custom_call" | custom-call | tf_op jit(solution)/shard_map/results/pallas_call | solution.py:626

commit v5 on v4

--- a/solution.py
+++ b/solution.py
@@ -13,6 +13,7 @@
 NN = (((1,), (0,)), ((), ()))
 NT = (((1,), (1,)), ((), ()))
 ROW0 = 8
+PARTS = 4
 EARLY = 16
 
 
@@ -243,13 +244,15 @@
     rows8 = lax.broadcasted_iota(I32, (8, 128), 0)
 
     barrier, n_greeted = greet(n_head, n_track)
+    part = n_x // PARTS
+    parts = range(0, n_x, part)
     pairs = [
         (foot_hbm, foot),
         (mag_hbm, mag),
         (pot_hbm.at[:, pl.ds(0, 1), :], lines.at[0]),
         (pot_hbm.at[:, pl.ds(n_y - 1, 1), :], lines.at[1]),
-        (pot_hbm, pot.at[all_x, inner, :]),
-        (src_hbm, src),
+        *[(pot_hbm.at[pl.ds(x, part), :, :], pot.at[pl.ds(x + 1, part), inner, :]) for x in parts],
+        *[(src_hbm.at[pl.ds(x, part), :, :], src.at[pl.ds(x, part), :, :]) for x in parts],
         (dk_hbm, dk),
         (temp_hbm, tidx),
         (prof_hbm, prof),
@@ -257,7 +260,9 @@
         (next_hbm, tnext),
     ]
     loads = [pltpu.make_async_copy(a, b, in_sem.at[i]) for i, (a, b) in enumerate(pairs)]
-    for copy in loads:
+    large = loads[4 : 4 + 2 * PARTS]
+    small = loads[4 + 2 * PARTS : -2]
+    for copy in loads[:-2]:
         copy.start()
 
     for side, there in enumerate((has_low_x, has_high_x)):
@@ -305,18 +310,25 @@
         target[1 : n_x + 1, ROW0 - 1 : ROW0, :] = rows_in[0]
         target[1 : n_x + 1, ROW0 + n_y : ROW0 + n_y + 1, :] = rows_in[1]
 
+    everyone = pl.ds(0, n_track - 1)
+    next_one = (head, lax.rem(track + 1, n_track))
+    all_asks = remote(ask.at[everyone], asked.at[everyone], ask_send, ask_recv, next_one)
+    all_answers = remote(answer.at[everyone], answered.at[everyone], ans_send, ans_recv, next_one)
+
     start_halo = [pot_hbm.at[0], pot_hbm.at[n_x - 1]], lines, pot, lines_in, halo_send, halo_recv
     start(halo(*start_halo))
 
     def send_ask(step, _):
         other = lax.rem(track + step, n_track)
-        remote(ask.at[other], asked.at[track], ask_send.at[other], ask_recv.at[track], (head, other)).start()
+        remote(ask.at[other], asked.at[track], ask_send, ask_recv, (head, other)).start()
         return 0
 
     lax.fori_loop(1, n_track, send_ask, 0)
     start(rim_copies(n_head, n_track, edge, rim, rim_send, rim_recv, False))
-    loads[4].wait()
-    loads[5].wait()
+    for copy in large:
+        copy.wait()
+    for copy in loads[-2:]:
+        copy.start()
 
     edge_rows = 32
 
@@ -361,14 +373,15 @@
     mid_halo = [mid.at[1, inner, :], mid.at[n_x, inner, :]], lines_mid, mid, lines_mid_in, mid_send, mid_recv
     sends = halo(*mid_halo)
     start(sends[:2])
-    for row in (0, n_y - edge_rows):
-        sweep_edge(pot, mid, row)
+    sweep_edge(pot, mid, 0)
     lines_mid[0] = mid[1 : n_x + 1, ROW0 : ROW0 + 1, :]
+    start(sends[2:3])
+    sweep_edge(pot, mid, n_y - edge_rows)
     lines_mid[1] = mid[1 : n_x + 1, ROW0 + n_y - 1 : ROW0 + n_y, :]
-    start(sends[2:])
+    start(sends[3:])
 
     sweep_inner(mid, pot)
-    loads[6].wait()
+    small[0].wait()
     kernels = []
     for odd in range(2):
         weights = jnp.zeros((8, 128), F32)
@@ -396,12 +409,7 @@
     sweep_edge(mid, pot, n_y - edge_rows, surface)
     surface(n_x // 8)
 
-    def wait_ask(step, _):
-        other = lax.rem(track + step, n_track)
-        remote(ask.at[other], asked.at[other], ask_send.at[other], ask_recv.at[other], (head, other)).wait_recv()
-        return 0
-
-    lax.fori_loop(1, n_track, wait_ask, 0)
+    all_asks.wait_recv()
     table = halves(surf[...])
 
     def reply(far_y, own):
@@ -418,7 +426,7 @@
             answered[track] = answer[track]
             others = others[:-1]
         for other in others:
-            remote(answer.at[other], answered.at[track], ans_send.at[other], ans_recv.at[track], (head, other)).start()
+            remote(answer.at[other], answered.at[track], ans_send, ans_recv, (head, other)).start()
 
     def reply_far(group, _):
         reply(jnp.where(group == 0, 2, jnp.where(group == 1, 1, 3)), False)
@@ -441,7 +449,7 @@
     state = [mag[comp] for comp in range(3)]
     for comp in range(3):
         set_lhs(1, state[comp], comp)
-    for copy in loads[7:]:
+    for copy in [*small[1:], *loads[-2:]]:
         copy.wait()
 
     def first_exchange(k, _):
@@ -464,12 +472,7 @@
     )
     target = 0.05 + jnp.maximum(1.0 - temp, 0.0)
 
-    def wait_answer(step, _):
-        other = lax.rem(track + step, n_track)
-        remote(answer.at[other], answered.at[other], ans_send.at[other], ans_recv.at[other], (head, other)).wait_recv()
-        return 0
-
-    lax.fori_loop(1, n_track, wait_answer, 0)
+    all_answers.wait_recv()
     table = halves(answered[...].reshape(8 * n_track, 128))
     applied = [[None] * n_tiles for _ in range(3)]
 
@@ -508,13 +511,8 @@
         set_lhs(1, state[comp], comp)
     lax.fori_loop(0, EARLY, next_exchange, 0, unroll=4)
 
-    def wait_sent(step, _):
-        other = lax.rem(track + step, n_track)
-        remote(ask.at[other], asked.at[other], ask_send.at[other], ask_recv.at[other], (head, other)).wait_send()
-        remote(answer.at[other], answered.at[other], ans_send.at[other], ans_recv.at[other], (head, other)).wait_send()
-        return 0
-
-    lax.fori_loop(1, n_track, wait_sent, 0)
+    all_asks.wait_send()
+    all_answers.wait_send()
     finish(halo_waits(*start_halo), True)
     finish(halo_waits(*mid_halo), True)
     finish(rim_copies(n_head, n_track, edge, rim, rim_send, rim_recv, True), True)
@@ -530,8 +528,15 @@
 ):
     n_x, n_y, _ = relaxed_hbm.shape
     n_tiles, width = target.shape
-    store = pltpu.make_async_copy(pot.at[pl.ds(1, n_x), pl.ds(ROW0, n_y), :], relaxed_hbm, sem.at[0])
-    store.start()
+    part = n_x // PARTS
+    stores = [
+        pltpu.make_async_copy(
+            pot.at[pl.ds(part * i + 1, part), pl.ds(ROW0, n_y), :], relaxed_hbm.at[pl.ds(part * i, part), :, :], sem.at[i]
+        )
+        for i in range(PARTS)
+    ]
+    for store in stores:
+        store.start()
     ex[0 : 8 * EARLY, :] = ex_early[0 : 8 * EARLY, :]
 
     def next_exchange(k, _):
@@ -551,10 +556,11 @@
     fields = [applied[comp] + e for comp, e in enumerate(get_ex(ex))]
     for comp, value in enumerate(llb_section(state, fields, target[...])):
         state_out[comp] = value
-    copy = pltpu.make_async_copy(state_out, magnet_hbm, sem.at[1])
+    copy = pltpu.make_async_copy(state_out, magnet_hbm, sem.at[PARTS])
     copy.start()
     copy.wait()
-    store.wait()
+    for store in stores:
+        store.wait()
 
 
 def per_device(n_head, n_track, potential, source, depth_kernel, magnet, footprint, temp_index, temp_profile, self_tiles, next_tiles):
@@ -613,10 +619,10 @@
             vmem((8 * (n_x // 2), n_y), F32),
             vmem((n_track, 8, width), F32),
             vmem((n_track, 8, width), F32),
-            dma((11,)),
+            dma((9 + 2 * PARTS,)),
             *[dma((4,))] * 4,
             *[dma((2,))] * 4,
-            *[dma((n_track,))] * 4,
+            *[dma] * 4,
         ],
         compiler_params=pltpu.CompilerParams(
             collective_id=0, has_side_effects=True, vmem_limit_bytes=24 << 20
@@ -628,7 +634,7 @@
         out_shape=(hbm(potential.shape, F32), hbm(grains, F32)),
         in_specs=[in_vmem] * len(shared),
         out_specs=(in_hbm, in_hbm),
-        scratch_shapes=[vmem((8 * n_tiles, width), F32), vmem(grains, F32), dma((2,))],
+        scratch_shapes=[vmem((8 * n_tiles, width), F32), vmem(grains, F32), dma((PARTS + 1,))],
         compiler_params=pltpu.CompilerParams(vmem_limit_bytes=4 << 20),
         name="results",
     )(*results)

time: 41.4 us -> 39.2 us (0.947)
  Pallas kernels: 40.6 us -> 38.4 us
    pallas_call x1, Pallas kernels: 38.5 us -> 36.3 us  [per_device(): pl.pallas_call(functools.partial(main_kernel, n_head, n_track), out_shape...]
where the time goes in v5:
time: 39.2 us; the launch traced here: 39 us
  Pallas kernels  38.4 us (98%)
  between operations  0.64 us (2%)
    pallas_call x1, Pallas kernels, per_device(): pl.pallas_call(functools.partial(main_kernel, n_head, n_track), out_shape...  36.3 us
    pallas_call x1, Pallas kernels, per_device(): pl.pallas_call(last_kernel, out_shape=(hbm(potential.shape, F32), hbm(gra...  2.06 us

profile of v5, /device:TPU:1, one launch (start us, length us, event | category | flops | bytes accessed | tf_op | source)
XLA Modules:
  0.0 39.0 jit_solution(13352136461407570108)
XLA Ops:
  0.6 36.3 %pole_and_grains.1 = (f32[66,144,128]{2,1,0:T(8,128)S(1)}, bf16[32,128,256]{2,1,0:T(8,128)(2,1)S(1)}, bf16[32,128,256]{2,1,0:T(8,128)(2,1)S(1)}, bf16[32,256,128...) custom-call(f32[64,128,128]{2,1,0:T(8,128)} %pot_hbm.1, ...), custom_call_target="tpu_custom_call" | custom-call | tf_op jit(solution)/shard_map/pole_and_grains/pallas_call | solution.py:598
  37.0 2.1 %results.1 = (f32[64,128,128]{2,1,0:T(8,128)}, f32[3,32,128]{2,1,0:T(8,128)}) custom-call(f32[66,144,128]{2,1,0:T(8,128)S(1)} %get-tuple-element.14.pot, bf16[32,128,256]{2,1,0:T(8,128)(2,1)S(1)} %get-tuple-element.15.near_high, bf16[32,128,256]{2,1,0:T(8,128)(2,1)S(1)} %get-tuple-element.16.near_low, bf16[32,256,128]{2,1,0:T(8,128)(2,1)S(1)} %get-tuple-element.17.above, ...), custom_call_target="tpu_custom_call" | custom-call | tf_op jit(solution)/shard_map/results/pallas_call | solution.py:632

commit v6 on v5

--- a/solution.py
+++ b/solution.py
@@ -14,7 +14,7 @@
 NT = (((1,), (1,)), ((), ()))
 ROW0 = 8
 PARTS = 4
-EARLY = 16
+EARLY = 24
 
 
 def mxu(a, b, dims):
@@ -353,7 +353,7 @@
         planes(1 + unroll * trips, n_x - 2 - unroll * trips, carried)
 
     def sweep_inner(source, target):
-        sweep_chunk(source, target, edge_rows, n_y - 2 * edge_rows, 4)
+        sweep_chunk(source, target, edge_rows, n_y - 2 * edge_rows, 8)
 
     def sweep_outer(source, target):
         for side, x in enumerate((0, n_x - 1)):

time: 39.2 us -> 39 us (level)
  no operation moved by 1% of the time
where the time goes in v6:
time: 39 us; the launch traced here: 38.9 us
  Pallas kernels  38.2 us (98%)
  between operations  0.64 us (2%)
    pallas_call x1, Pallas kernels, per_device(): pl.pallas_call(functools.partial(main_kernel, n_head, n_track), out_shape...  36.2 us
    pallas_call x1, Pallas kernels, per_device(): pl.pallas_call(last_kernel, out_shape=(hbm(potential.shape, F32), hbm(gra...  2.06 us

profile of v6, /device:TPU:1, one launch (start us, length us, event | category | flops | bytes accessed | tf_op | source)
XLA Modules:
  0.0 38.9 jit_solution(8302131598602805016)
XLA Ops:
  0.6 36.2 %pole_and_grains.1 = (f32[66,144,128]{2,1,0:T(8,128)S(1)}, bf16[32,128,256]{2,1,0:T(8,128)(2,1)S(1)}, bf16[32,128,256]{2,1,0:T(8,128)(2,1)S(1)}, bf16[32,256,128...) custom-call(f32[64,128,128]{2,1,0:T(8,128)} %pot_hbm.1, ...), custom_call_target="tpu_custom_call" | custom-call | tf_op jit(solution)/shard_map/pole_and_grains/pallas_call | solution.py:598
  36.8 2.1 %results.1 = (f32[64,128,128]{2,1,0:T(8,128)}, f32[3,32,128]{2,1,0:T(8,128)}) custom-call(f32[66,144,128]{2,1,0:T(8,128)S(1)} %get-tuple-element.14.pot, bf16[32,128,256]{2,1,0:T(8,128)(2,1)S(1)} %get-tuple-element.15.near_high, bf16[32,128,256]{2,1,0:T(8,128)(2,1)S(1)} %get-tuple-element.16.near_low, bf16[32,256,128]{2,1,0:T(8,128)(2,1)S(1)} %get-tuple-element.17.above, ...), custom_call_target="tpu_custom_call" | custom-call | tf_op jit(solution)/shard_map/results/pallas_call | solution.py:632

commit v7 on v6

--- a/solution.py
+++ b/solution.py
@@ -364,7 +364,7 @@
                 target[x + 1, rows, :], _ = swept(source, src, faces, slot, x, row, edge_rows, carried)
 
     def sweep_edge(source, target, row, beside=None):
-        sweep_chunk(source, target, row, edge_rows, 8, beside)
+        sweep_chunk(source, target, row, edge_rows, 8 if beside else 16, beside)
 
     sweep_inner(pot, mid)
     finish(halo_waits(*start_halo), False)
@@ -603,7 +603,7 @@
         scratch_shapes=[
             vmem(padded, F32),
             vmem((n_x, n_y, n_z), F32),
-            vmem((2, 8, n_y, n_z), F32),
+            vmem((2, 16, n_y, n_z), F32),
             vmem((3, n_z), F32),
             vmem(grains, F32),
             vmem((n_tiles, width), I32),

time: 39 us -> 38.9 us (level)
  no operation moved by 1% of the time
where the time goes in v7:
time: 38.9 us; the launch traced here: 38.8 us
  Pallas kernels  38.1 us (98%)
  between operations  0.64 us (2%)
    pallas_call x1, Pallas kernels, per_device(): pl.pallas_call(functools.partial(main_kernel, n_head, n_track), out_shape...  36.1 us
    pallas_call x1, Pallas kernels, per_device(): pl.pallas_call(last_kernel, out_shape=(hbm(potential.shape, F32), hbm(gra...  2.06 us

profile of v7, /device:TPU:1, one launch (start us, length us, event | category | flops | bytes accessed | tf_op | source)
XLA Modules:
  0.0 38.8 jit_solution(3869725317875611813)
XLA Ops:
  0.6 36.1 %pole_and_grains.1 = (f32[66,144,128]{2,1,0:T(8,128)S(1)}, bf16[32,128,256]{2,1,0:T(8,128)(2,1)S(1)}, bf16[32,128,256]{2,1,0:T(8,128)(2,1)S(1)}, bf16[32,256,128...) custom-call(f32[64,128,128]{2,1,0:T(8,128)} %pot_hbm.1, ...), custom_call_target="tpu_custom_call" | custom-call | tf_op jit(solution)/shard_map/pole_and_grains/pallas_call | solution.py:598
  36.7 2.1 %results.1 = (f32[64,128,128]{2,1,0:T(8,128)}, f32[3,32,128]{2,1,0:T(8,128)}) custom-call(f32[66,144,128]{2,1,0:T(8,128)S(1)} %get-tuple-element.14.pot, bf16[32,128,256]{2,1,0:T(8,128)(2,1)S(1)} %get-tuple-element.15.near_high, bf16[32,128,256]{2,1,0:T(8,128)(2,1)S(1)} %get-tuple-element.16.near_low, bf16[32,256,128]{2,1,0:T(8,128)(2,1)S(1)} %get-tuple-element.17.above, ...), custom_call_target="tpu_custom_call" | custom-call | tf_op jit(solution)/shard_map/results/pallas_call | solution.py:632
